TPU v7x, 256 devices: a whole 4x4x8 slice. The times are simulated.
256 devices in a mesh: ctx: 64 (over z, y_lo, x), head: 4 (over y_hi, core).
Axes of the slice: x: 4, y: 4 (y_hi: 2, y_lo: 2; y = y_hi * 2 + y_lo), z: 8, core: 2. Of those that a mesh axis runs over, the one named last changes fastest.
Arguments:
- queries: bfloat16 [8192, 1024], P('ctx', 'head'), may hold values from -27 to 27
- keys: bfloat16 [8192, 128], P('ctx'), may hold values from -4 to 4
- values: bfloat16 [8192, 128], P('ctx'), may hold values from -6 to 6
- dout: bfloat16 [8192, 1024], P('ctx', 'head'), may hold values from -6 to 6
- positions: int32 [8192], P('ctx'), may hold values from 0 to 8191, as said below
- doc_ids: int32 [8192], P('ctx'), may hold values from 0 to 127, as said below
- w_query: bfloat16 [1024, 16384], P('head'), may hold values from -0.1875 to 0.1875
- w_kv: bfloat16 [256, 16384], P(None, 'head'), may hold values from -0.375 to 0.375
Outputs:
- grad_input: bfloat16 [8192, 16384], P('ctx', 'head')
Inputs may be any that keep to these rules, and one draw needn't show every extreme that they name: Stored rows come in aligned runs of 64 rows that hold 64 consecutive positions in order, starting at a multiple of 64; every position of the sequence is stored once. `doc_ids`: A document is a set of consecutive positions that begins at a multiple of 64; its id is its first position divided by 64. The first and the last run of 64 positions each begin a document.
All inputs are finite; a program needn't handle non-finite values.
Results may differ from a plain program's by a relative error of at most 0.019.
Values may be sent and summed in bfloat16 or wider, within the bound.
A program may use at most 128 MiB of HBM per device.

v0:
```python
import math

import jax
import jax.numpy as jnp
from jax import lax
from jax.sharding import Mesh
from jax.sharding import PartitionSpec as P

CTX = ("ctx_0", "ctx_1", "ctx_2")


def side_by_side(arrays, axis, dim, along):
    ends, at = ([], 0)
    for a in arrays[:-1]:
        at += a.shape[along]
        ends.append(at)
    both = jnp.concatenate(arrays, axis=along)
    return tuple(jnp.split(lax.all_gather(both, axis, axis=dim, tiled=True), ends, axis=along))


def reduced_to_own(parts, axes, turns):
    inside = parts.shape[1:]
    parts = parts.reshape(*(lax.axis_size(a) for a in axes), *inside)
    parts = jnp.moveaxis(parts, turns, range(len(axes))).reshape(-1, *inside)
    for k in turns:
        parts = lax.psum_scatter(parts, axes[k], scatter_dimension=0, tiled=True)
    return parts[0]


def cut_along(value, dim, length):
    before, after = (value.shape[:dim], value.shape[dim + 1 :])
    return jnp.moveaxis(value.reshape(*before, length, -1, *after), dim, 0)


def sum_by_axis(value, axes, turns, dim):
    length = lax.axis_size(axes)
    return reduced_to_own(cut_along(value, dim, length), axes, turns)


def from_everyone(value, axis):
    copies = jnp.broadcast_to(value, (lax.axis_size(axis), *value.shape))
    return lax.all_to_all(copies, axis, split_axis=0, concat_axis=0, tiled=True)


def over_copies(value, axis):
    everything = from_everyone(value, axis)
    return jnp.sum(everything.astype(jnp.float32), axis=0)


def on_device(queries, keys, values, dout, positions, doc_ids, w_query, w_kv):
    head_size = keys.shape[1]
    tok_rows = queries.shape[0]
    local_heads = queries.shape[1] // head_size
    inv_root = 1.0 / math.sqrt(head_size)
    query_rows = queries.reshape(tok_rows, local_heads, head_size)
    dout_rows = dout.reshape(tok_rows, local_heads, head_size)

    def allowed_pairs(pos_piece, doc_piece):
        return (doc_ids[:, None] == doc_piece[None, :]) & (pos_piece[None, :] <= positions[:, None])

    def block_scores(key_piece):
        return (
            jnp.einsum("qhd,kd->hqk", query_rows, key_piece, preferred_element_type=jnp.float32)
            * inv_root
        )

    def fold_keys(totals, shard_piece):
        key_piece, value_piece, pos_piece, doc_piece = shard_piece
        allowed = allowed_pairs(pos_piece, doc_piece)
        row_max, row_total, weighted = totals
        masked = jnp.where(allowed[None], block_scores(key_piece), -1e30)
        new_max = jnp.maximum(row_max, jnp.max(masked, axis=-1))
        probs = jnp.where(allowed[None], jnp.exp(masked - new_max[..., None]), 0.0)
        factor = jnp.exp(row_max - new_max)
        mixed = jnp.einsum("hqk,kd->hqd", probs, value_piece.astype(jnp.float32))
        return (
            new_max,
            row_total * factor + jnp.sum(probs, axis=-1),
            weighted * factor[..., None] + mixed,
        )

    initial = (
        jnp.full((local_heads, tok_rows), -1e30, jnp.float32),
        jnp.zeros((local_heads, tok_rows), jnp.float32),
        jnp.zeros((local_heads, tok_rows, head_size), jnp.float32),
    )

    def grad_terms(key_piece, value_piece, allowed, log_total, row_delta):
        probs = jnp.where(
            allowed[None], jnp.exp(block_scores(key_piece) - log_total[..., None]), 0.0
        )
        probs_low = probs.astype(jnp.bfloat16)
        value_term = jnp.einsum(
            "hqk,qhd->kd", probs_low, dout_rows, preferred_element_type=jnp.float32
        )
        dprob = jnp.einsum(
            "qhd,kd->hqk", dout_rows, value_piece, preferred_element_type=jnp.float32
        )
        dscore = (probs * (dprob - row_delta[..., None])).astype(jnp.bfloat16)
        query_term = jnp.einsum(
            "hqk,kd->qhd", dscore, key_piece, preferred_element_type=jnp.float32
        )
        key_term = jnp.einsum("hqk,qhd->kd", dscore, query_rows, preferred_element_type=jnp.float32)
        return (query_term, jnp.concatenate([key_term, value_term], axis=1))

    all_k, all_v, all_pos, all_doc = (
        *side_by_side((keys, values), CTX, 0, 1),
        lax.all_gather(positions, CTX, axis=0, tiled=True),
        lax.all_gather(doc_ids, CTX, axis=0, tiled=True),
    )
    seq_rows = all_k.shape[0]
    block_rows = math.gcd(seq_rows, 512)
    block_count = seq_rows // block_rows

    def pieces_at(number):
        start_row = number * block_rows
        return tuple(
            (
                lax.dynamic_slice_in_dim(whole, start_row, block_rows, 0)
                for whole in (all_k, all_v, all_pos, all_doc)
            )
        )

    def forward_block(totals, number):
        return (fold_keys(totals, pieces_at(number)), None)

    numbers = jnp.arange(block_count, dtype=jnp.int32)
    totals, unused = lax.scan(forward_block, initial, numbers)
    row_max, row_total, weighted = totals
    finish_log_total = row_max + jnp.log(row_total)
    output = weighted / row_total[..., None]
    finish_row_delta = jnp.einsum("qhd,hqd->hq", dout_rows.astype(jnp.float32), output)
    log_total = finish_log_total
    row_delta = finish_row_delta

    def backward_block(query_total, number):
        key_piece, value_piece, pos_piece, doc_piece = pieces_at(number)
        allowed = allowed_pairs(pos_piece, doc_piece)
        query_term, kv_term = grad_terms(key_piece, value_piece, allowed, log_total, row_delta)
        return (query_total + query_term, kv_term)

    query_total, kv_blocks = lax.scan(
        backward_block, jnp.zeros((tok_rows, local_heads, head_size), jnp.float32), numbers
    )
    kv_total = sum_by_axis(kv_blocks.reshape(seq_rows, 2 * head_size), CTX, (0, 2, 1), 0)
    kv_total = over_copies(kv_total.astype(jnp.bfloat16), "head").astype(jnp.float32)
    column_scale = jnp.where(jnp.arange(2 * head_size) < head_size, inv_root, 1.0).astype(
        jnp.float32
    )
    kv_grads = (kv_total * column_scale[None, :]).astype(jnp.bfloat16)
    query_grad = (
        (query_total * inv_root).astype(jnp.bfloat16).reshape(tok_rows, local_heads * head_size)
    )
    kv_part = jnp.dot(kv_grads, w_kv, preferred_element_type=jnp.float32)
    whole_width = jnp.dot(query_grad, w_query, preferred_element_type=jnp.float32)
    query_part = lax.psum_scatter(
        whole_width.astype(jnp.bfloat16), "head", scatter_dimension=1, tiled=True
    ).astype(jnp.float32)
    return (query_part + kv_part).astype(jnp.bfloat16)


def solution(mesh):
    torus = Mesh(
        mesh.devices.reshape(8, 2, 4, mesh.shape["head"]), ("ctx_0", "ctx_1", "ctx_2", "head")
    )
    return jax.shard_map(
        on_device,
        mesh=torus,
        in_specs=(
            P(CTX, "head"),
            P(CTX, None),
            P(CTX, None),
            P(CTX, "head"),
            P(CTX),
            P(CTX),
            P("head", None),
            P(None, "head"),
        ),
        out_specs=P(CTX, "head"),
        check_vma=False,
    )
```

profile of v0, /device:TPU:1, one launch (start us, length us, event | category | flops | bytes accessed | tf_op | source)
XLA Modules:
  0.0 712.6 jit_solution(6676892114939235245)
XLA Ops:
  6.5 1.6 pad_maximum_fusion
  10.3 133.0 %all-gather = s32[64,1,128]{2,1,0:T(1,128)S(1)} all-gather(s32[1,1,128]{2,1,0:T(1,128)} %bitcast.124), channel_id=1, replica_groups=mesh['ctx_0'=8,'ctx_1'=2,'ctx_2'=4,'head'=4] {'ctx_0','ctx_1','ctx_2'}, dimensions={0}, use_global_device_ids=true | all-gather | bytes 33280 | tf_op jit(solution)/shard_map/all_gather | solution.py:109
  143.3 124.3 %all-gather.1 = s32[64,1,128]{2,1,0:T(1,128)S(1)} all-gather(s32[1,1,128]{2,1,0:T(1,128)} %bitcast.125), channel_id=1, replica_groups=mesh['ctx_0'=8,'ctx_1'=2,'ctx_2'=4,'head'=4] {'ctx_0','ctx_1','ctx_2'}, dimensions={0}, use_global_device_ids=true | all-gather | bytes 33280 | tf_op jit(solution)/shard_map/all_gather | solution.py:108
  267.6 2.5 all-gather.4.cloned.1.call-done
  270.1 4.4 fusion.36
  274.6 67.4 %while.28 = (s32[]{:T(128)}, f32[2,128]{1,0:T(2,128)S(1)}, f32[2,128]{1,0:T(2,128)S(1)}, f32[2,128,128]{2,1,0:T(8,128)S(1)}, s32[128]{0:T(128)S(1)}, /*index=5*/...) while((s32[]{:T(128)}, f32[2,128]{1,0:T(2,128)S(1)}, ...), condition=%wide.region_3.4_spmd.clone, body=%wide.region_0.3_spmd.clone.sunk | while | flops 68453632 | bytes 2454771 | solution.py:128
  276.2 1.2 fusion.68
  277.5 1.2 convolution_add_fusion.3
  280.4 1.2 fusion.68
  281.8 1.2 convolution_add_fusion.3
  284.6 1.2 fusion.68
  286.0 1.2 convolution_add_fusion.3
  288.8 1.2 fusion.68
  290.2 1.2 convolution_add_fusion.3
  293.1 1.2 fusion.68
  294.4 1.2 convolution_add_fusion.3
  297.3 1.2 fusion.68
  298.6 1.2 convolution_add_fusion.3
  301.5 1.2 fusion.68
  302.8 1.2 convolution_add_fusion.3
  305.7 1.2 fusion.68
  307.0 1.2 convolution_add_fusion.3
  309.9 1.2 fusion.68
  311.3 1.2 convolution_add_fusion.3
  314.1 1.2 fusion.68
  315.5 1.2 convolution_add_fusion.3
  318.3 1.2 fusion.68
  319.7 1.2 convolution_add_fusion.3
  322.6 1.2 fusion.68
  323.9 1.2 convolution_add_fusion.3
  326.8 1.2 fusion.68
  328.1 1.2 convolution_add_fusion.3
  331.0 1.2 fusion.68
  332.3 1.2 convolution_add_fusion.3
  335.2 1.2 fusion.68
  336.5 1.2 convolution_add_fusion.3
  339.4 1.2 fusion.68
  340.8 1.2 convolution_add_fusion.3
  342.3 105.8 %while.29 = (s32[]{:T(128)}, f32[128,2,128]{0,2,1:T(8,128)S(1)}, f32[16,512,256]{2,1,0:T(8,128)}, s32[16]{0:T(128)S(1)}, bf16[8192,128]{1,0:T(8,128)(2,1)}, /*in...) while((s32[]{:T(128)}, f32[128,2,128]{0,2,1:T(8,128)S(1)}, ...), condition=%wide.region_5.6_spmd.clone, body=%wide.region_4.5_spmd.clone.sunk | while | flops 169082880 | bytes 7093513 | solution.py:142
  346.2 1.2 fusion.84
  352.8 1.2 fusion.84
  359.4 1.2 fusion.84
  366.0 1.2 fusion.84
  372.6 1.2 fusion.84
  379.2 1.2 fusion.84
  385.9 1.2 fusion.84
  392.5 1.2 fusion.84
  399.1 1.2 fusion.84
  405.7 1.2 fusion.84
  412.3 1.2 fusion.84
  418.9 1.2 fusion.84
  425.5 1.2 fusion.84
  432.2 1.2 fusion.84
  438.8 1.2 fusion.84
  445.4 1.2 fusion.84
  448.1 7.6 %copy.64 = f32[8,4,2,128,256]{4,3,2,1,0:T(8,128)} copy(f32[8,4,2,128,256]{4,3,1,2,0:T(8,128)} %bitcast.118) | data formatting | bytes 16777216 | tf_op jit(solution)/shard_map/transpose | solution.py:24
  455.8 141.2 %reduce-scatter.7.cloned.1.call-done = f32[8,128,256]{2,1,0:T(8,128)} async-done(((f32[64,128,256]{2,1,0:T(8,128)}), f32[8,128,256]{2,1,0:T(8,128)}) %reduce-scatter.7.cloned.1.call-update) | async-done | bytes 1048592 | tf_op jit(solution)/shard_map/reduce_scatter | solution.py:26
  597.0 26.0 %reduce-scatter.9.cloned.1.call-done = f32[2,128,256]{2,1,0:T(8,128)} async-done(((f32[8,128,256]{2,1,0:T(8,128)}), f32[2,128,256]{2,1,0:T(8,128)}) %reduce-scatter.9.cloned.1.call-update) | async-done | bytes 262160 | tf_op jit(solution)/shard_map/reduce_scatter | solution.py:26
  623.1 6.6 convolution_convert_fusion
  629.7 13.5 %reduce-scatter.11.cloned.1.call-done = f32[1,128,256]{2,1,0:T(8,128)} async-done(((f32[2,128,256]{2,1,0:T(8,128)}), f32[1,128,256]{2,1,0:T(8,128)}) %reduce-scatter.11.cloned.1.call-update) | async-done | bytes 131088 | tf_op jit(solution)/shard_map/reduce_scatter | solution.py:26
  644.9 4.8 all-to-all-start
  649.7 6.5 all-to-all-done
  656.3 47.2 %reduce-scatter.5.cloned.1.call-done = bf16[128,4096]{1,0:T(8,128)(2,1)} async-done(((bf16[128,16384]{1,0:T(8,128)(2,1)}), bf16[128,4096]{1,0:T(8,128)(2,1)}) %reduce-scatter.5.cloned.1.call-update) | async-done | bytes 1048592 | tf_op jit(solution)/shard_map/reduce_scatter | solution.py:156
  703.4 2.6 fusion.33
  (339 shorter events, 97.3 us)
Async XLA Ops:
  6.5 696.9 %copy-start = (bf16[256,4096]{1,0:T(8,128)(2,1)S(1)}, bf16[256,4096]{1,0:T(8,128)(2,1)}, u32[]{:S(2)}) copy-start(bf16[256,4096]{1,0:T(8,128)(2,1)} %param.19) | copy-start | bytes 6291460
  6.5 263.6 %all-gather.4.cloned.1.call-start = ((), (), s32[]{:S(2)}) async-start(), calls=%async_computation.5 | async-start | bytes 4259840 | tf_op jit(solution)/shard_map/all_gather | solution.py:18
  8.1 588.8 %reduce-scatter.7.cloned.1.call-start = ((), (), s32[]{:S(2)}) async-start(), calls=%async_computation.7 | async-start | bytes 9437184 | tf_op jit(solution)/shard_map/reduce_scatter | solution.py:26
  267.6 7.0 copy-start.1
  267.6 7.0 copy-start.2
  455.7 167.3 %reduce-scatter.9.cloned.1.call-start = ((), (), s32[]{:S(2)}) async-start(), calls=%async_computation.8 | async-start | bytes 1310720 | tf_op jit(solution)/shard_map/reduce_scatter | solution.py:26
  597.0 46.3 %reduce-scatter.11.cloned.1.call-start = ((), (), s32[]{:S(2)}) async-start(), calls=%async_computation.9 | async-start | bytes 393216 | tf_op jit(solution)/shard_map/reduce_scatter | solution.py:26
  623.0 80.4 %reduce-scatter.5.cloned.1.call-start = ((), (), s32[]{:S(2)}) async-start(), calls=%async_computation.6 | async-start | bytes 5242880 | tf_op jit(solution)/shard_map/reduce_scatter | solution.py:156
  644.9 11.4 %all-to-all-start = ((bf16[4,128,256]{2,1,0:T(8,128)(2,1)}), bf16[4,128,256]{2,1,0:T(8,128)(2,1)S(1)}, u32[]{:S(2)}, u32[]{:S(2)}) async-start(bf16[4,128,256]{2,1,0:T(8,128)(2,1)} %broadcast_in_dim.78), calls=%async_computation.4 | async-start | bytes 524288 | tf_op jit(solution)/shard_map/all_to_all | solution.py:42
Sparse Core Ops, SparseCore 0:
  9.1 260.9 all-gather.3
  455.8 141.0 reduce-scatter.6
  599.5 23.4 reduce-scatter.8
  625.3 17.8 reduce-scatter.10
  645.9 57.5 reduce-scatter.4
where the time goes:
time: 715 us; the launch traced here: 713 us
  blocking collectives  257 us (36%)
  waiting for transfers between devices  237 us (33%)
  matrix products  110 us (15%)
  local copies, waits for them, and re-layouts  55 us (8%)
  loops' own time  23 us (3%)
  between operations  13.3 us (2%)
  other arithmetic  12.1 us (2%)
    reduce_scatter x3, waiting for transfers between devices, reduced_to_own(): parts = lax.psum_scatter(parts, axes[k], scatter_dimension=0, tiled=True)  181 us
    all_gather x1, blocking collectives, on_device(): lax.all_gather(doc_ids, CTX, axis=0, tiled=True)  133 us
    all_gather x1, blocking collectives, on_device(): lax.all_gather(positions, CTX, axis=0, tiled=True)  124 us
    reduce_scatter x1, waiting for transfers between devices, on_device(): lax.psum_scatter(whole_width.astype(jnp.bfloat16), 'head', scatter_dimens...  47.2 us
    dot_general x32, matrix products, block_scores(): jnp.einsum('qhd,kd->hqk', query_rows, key_piece, preferred_element_type=j...  37.1 us
    dot_general x16, matrix products, fold_keys(): mixed = jnp.einsum('hqk,kd->hqd', probs, value_piece.astype(jnp.float32))  19.9 us
    dynamic_slice x32, local copies, waits for them, and re-layouts, on_device(): totals, unused = lax.scan(forward_block, initial, numbers)  18.7 us
    dot_general x16, matrix products, grad_terms(): jnp.einsum('hqk,kd->qhd', dscore, key_piece, preferred_element_type=jnp.f...  18.6 us
  transfers between devices with their start and end apart: 6, of which 6 were waited for; matrix products, arithmetic and copies ran while one was open for 1% of the time, Pallas kernels for 0%

commit v1 on v0

v1 whole, which is shorter than its diff:
```python
import math

import jax
import jax.numpy as jnp
from jax import lax
from jax.experimental import pallas as pl
from jax.experimental.pallas import tpu as pltpu
from jax.sharding import Mesh
from jax.sharding import PartitionSpec as P

CTX = ("z", "yl", "x")
HEAD = ("u", "c")
MESH = pl.DeviceIdType.MESH
BF = jnp.bfloat16
F32 = jnp.float32
NEG = -1e30
INV = 1.0 / math.sqrt(128)
LOG2E = 1.4426950408889634
NT = (((1,), (1,)), ((), ()))
NN = (((1,), (0,)), ((), ()))


def mm(a, b, dims=NN):
    return lax.dot_general(a, b, dims, preferred_element_type=F32)


def kernel(
    pos, doc, q, do, k, v, wq, wkv, out,
    Q, DO, KA, V, KT, MQ, MK, meta, tri, S, DP, stat, mloc, stat_all, coef,
    dk, dv, dqs, dqr, pair_s, pair_r, zs, zr, hs, hr, dqf, dqx, W, WK, part_s, part_r,
    q_s, q_r, d_s, d_r, k_s, k_r, v_s, v_r, mq_s, mq_r, mk_s, mk_r, st_s, st_r,
    dq_s, dq_r, z_s, z_r, pr_s, pr_r, h_s, h_r, x_s, x_r, w_s, w_r, pt_s, pt_r, loc,
):
    z, yl, x = lax.axis_index("z"), lax.axis_index("yl"), lax.axis_index("x")
    u, c = lax.axis_index("u"), lax.axis_index("c")
    p = yl * 4 + x

    def plane(d):
        t = (p + d + 8) % 8
        return (z, t // 4, t % 4, u, c)

    def ring(d):
        return ((z + d + 8) % 8, yl, x, u, c)

    mate = (z, yl, x, u, 1 - c)
    side = (z, 1 - yl, x, u, c)
    side_mate = (z, 1 - yl, x, u, 1 - c)
    far = (z, yl, x, 1 - u, c)
    far_mate = (z, yl, x, 1 - u, 1 - c)
    cross = (z, 1 - yl, x, 1 - u, c)

    def rc(src, dst, ss, rs, dev):
        return pltpu.make_async_remote_copy(
            src_ref=src, dst_ref=dst, send_sem=ss, recv_sem=rs, device_id=dev, device_id_type=MESH
        )

    def cols(uu, cc):
        return pl.ds(pl.multiple_of((2 * uu + cc) * 4096, 4096), 4096)

    own = [
        pltpu.make_async_copy(q, Q.at[0], loc.at[0]),
        pltpu.make_async_copy(do, DO.at[0], loc.at[1]),
        pltpu.make_async_copy(k, KA.at[pl.ds(0, 128), pl.ds(0, 128)], loc.at[2]),
        pltpu.make_async_copy(v, V.at[pl.ds(0, 128)], loc.at[3]),
        pltpu.make_async_copy(wq.at[:, cols(u, c)], W.at[pl.ds(0, 256), pl.ds(0, 4096)], loc.at[4]),
        pltpu.make_async_copy(
            wq.at[:, cols(1 - u, c)], W.at[pl.ds(0, 256), pl.ds(4096, 4096)], loc.at[5]
        ),
        pltpu.make_async_copy(wkv, WK, loc.at[6]),
    ]

    lane = lax.broadcasted_iota(jnp.int32, (1, 128), 1)
    r0, r1 = pos[0] // 64, pos[64] // 64
    s0, s1 = doc[0], doc[64]
    rows = [
        jnp.where((lane >= s0) & (lane <= r0), 0.0, NEG),
        jnp.where((lane >= s1) & (lane <= r1), 0.0, NEG),
        jnp.where(lane == r0, 1.0, 0.0),
        jnp.where(lane == r1, 1.0, 0.0),
        jnp.zeros((4, 128), F32),
    ]
    meta_val = jnp.concatenate(rows, axis=0)
    meta[...] = meta_val
    MQ[0] = meta_val
    MK[0] = meta_val
    jj = lax.broadcasted_iota(jnp.int32, (128, 256), 0)
    ii = lax.broadcasted_iota(jnp.int32, (128, 256), 1) % 128
    tri[...] = jnp.where((jj // 64 == ii // 64) & (jj > ii), NEG, 0.0)

    barrier = pltpu.get_barrier_semaphore()
    peers = [plane(d) for d in range(1, 8)] + [ring(d) for d in range(1, 8)]
    peers += [mate, side_mate, far, far_mate, cross]
    for dev in peers:
        pl.semaphore_signal(barrier, inc=1, device_id=dev, device_id_type=MESH)
    for cp in own[:4]:
        cp.start()
    pl.semaphore_wait(barrier, len(peers))

    ORDER = (1, 7, 2, 6, 3, 5, 4)
    gk = {d: rc(k, KA.at[pl.ds(d * 128, 128), pl.ds(0, 128)], k_s.at[d], k_r.at[d], ring(d)) for d in ORDER}
    gv = {d: rc(v, V.at[pl.ds(d * 128, 128)], v_s.at[d], v_r.at[d], ring(d)) for d in ORDER}
    gmk = {d: rc(meta, MK.at[d], mk_s.at[d], mk_r.at[d], ring(d)) for d in ORDER}
    gq = {d: rc(q, Q.at[d], q_s.at[d], q_r.at[d], plane(d)) for d in ORDER}
    gd = {d: rc(do, DO.at[d], d_s.at[d], d_r.at[d], plane(d)) for d in ORDER}
    gmq = {d: rc(meta, MQ.at[d], mq_s.at[d], mq_r.at[d], plane(d)) for d in ORDER}
    for d in ORDER:
        gmk[d].start()
        gk[d].start()
        gv[d].start()
        gmq[d].start()
        gq[d].start()
        gd[d].start()
    wpush = [
        rc(wq.at[:, cols(u, 1 - c)], W.at[pl.ds(256, 256), pl.ds(0, 4096)], w_s.at[0], w_r.at[0], mate),
        rc(wq.at[:, cols(1 - u, 1 - c)], W.at[pl.ds(256, 256), pl.ds(4096, 4096)], w_s.at[1], w_r.at[1], mate),
    ]
    for cp in wpush:
        cp.start()
    for cp in own[4:]:
        cp.start()

    def runs(ref, d, row):
        a = jnp.broadcast_to(ref[d, row : row + 1, :], (64, 128))
        b = jnp.broadcast_to(ref[d, row + 1 : row + 2, :], (64, 128))
        return jnp.concatenate([a, b], axis=0).astype(BF)

    for cp in own[:4]:
        cp.wait()
    for d in range(8):
        if d:
            gmk[d].wait_recv()
            gk[d].wait_recv()
            gv[d].wait_recv()
        at = pl.ds(d * 128, 128)
        KA[at, 128:256] = runs(MK, d, 2)
        KT[:, d * 128 : (d + 1) * 128] = KA[at, 0:128].astype(F32).T.astype(BF)

    def stacked(ref, d):
        return jnp.concatenate([ref[d, :, 0:128], ref[d, :, 128:256]], axis=0)

    def fold(val, op):
        return op(val.reshape(32, 8, 256), axis=0)

    def first(d, carry):
        @pl.when(d > 0)
        def _():
            rc(meta, MQ.at[d], mq_s.at[d], mq_r.at[d], plane(d)).wait_recv()
            rc(q, Q.at[d], q_s.at[d], q_r.at[d], plane(d)).wait_recv()
            rc(do, DO.at[d], d_s.at[d], d_r.at[d], plane(d)).wait_recv()

        bias = runs(MQ, d, 0)
        qa = jnp.concatenate(
            [stacked(Q, d), jnp.concatenate([bias, bias], axis=0)], axis=1
        )
        dd = stacked(DO, d)
        own_tile = jnp.where(d == 0, 1.0, 0.0)
        top = jnp.full((8, 256), -3e38, F32)
        for n in range(4):
            at = pl.ds(n * 256, 256)
            s = mm(KA[at, :], qa, NT)
            if n == 0:
                s = jnp.concatenate([s[0:128] + tri[...] * own_tile, s[128:256]], axis=0)
            S[d, at, :] = s
            top = jnp.maximum(top, fold(s, jnp.max))
            DP[d, at, :] = mm(V[at, :], dd, NT)
        m = jnp.max(top, axis=0, keepdims=True)
        mc = m * (INV * LOG2E)
        total = jnp.zeros((8, 256), F32)
        mixed = jnp.zeros((8, 256), F32)
        for n in range(4):
            at = pl.ds(n * 256, 256)
            e = jnp.exp2(S[d, at, :] * (INV * LOG2E) - mc)
            S[d, at, :] = e
            total = total + fold(e, jnp.sum)
            mixed = mixed + fold(e * DP[d, at, :], jnp.sum)
        total = jnp.sum(total, axis=0, keepdims=True)
        mixed = jnp.sum(mixed, axis=0, keepdims=True)
        mloc[pl.ds(d, 1), :] = m * INV
        stat[0, pl.ds(d, 1), :] = m * INV + jnp.log(total)
        stat[1, pl.ds(d, 1), :] = mixed / total
        return carry

    lax.fori_loop(0, 8, first, 0)

    gs = {d: rc(stat, stat_all.at[d], st_s.at[d], st_r.at[d], plane(d)) for d in ORDER}
    for d in ORDER:
        gs[d].start()
    lses, deltas = [stat[0]], [stat[1]]
    for d in range(1, 8):
        gs[d].wait_recv()
        for row, into in ((0, lses), (1, deltas)):
            a = stat_all[d, row]
            into.append(jnp.concatenate([a[8 - d :], a[: 8 - d]], axis=0))
    big = lses[0]
    for a in lses[1:]:
        big = jnp.maximum(big, a)
    tot = jnp.zeros((8, 256), F32)
    mix = jnp.zeros((8, 256), F32)
    for a, b in zip(lses, deltas):
        w = jnp.exp(a - big)
        tot = tot + w
        mix = mix + w * b
    coef[0] = jnp.exp(mloc[...] - (big + jnp.log(tot)))
    coef[1] = mix / tot

    dk[...] = jnp.zeros_like(dk)
    dv[...] = jnp.zeros_like(dv)

    def second(d, carry):
        f = coef[0, pl.ds(d, 1), :]
        delta = coef[1, pl.ds(d, 1), :]
        qq = stacked(Q, d)
        dd = stacked(DO, d)
        dqt = jnp.zeros((128, 256), F32)
        for n in range(4):
            at = pl.ds(n * 256, 256)
            pn = S[d, at, :] * f
            ds = (pn * (DP[d, at, :] - delta)).astype(BF)
            dv[at, :] += mm(pn.astype(BF), dd)
            dk[at, :] += mm(ds, qq)
            dqt = dqt + mm(KT[:, n * 256 : (n + 1) * 256], ds)
        dqs[d] = dqt.T.astype(BF)

        @pl.when(d > 0)
        def _():
            rc(dqs.at[d], dqr.at[d], dq_s.at[d], dq_r.at[d], plane(-d)).start()

        return carry

    lax.fori_loop(0, 8, second, 0)

    first_core = c == 0
    pair_s[...] = jnp.where(first_core, dv[...], dk[...]).astype(BF)
    pair = rc(pair_s, pair_r, pr_s, pr_r, mate)
    pair.start()

    dqsum = dqs[0].astype(F32)
    for d in range(1, 8):
        rc(dqs.at[d], dqr.at[d], dq_s.at[d], dq_r.at[d], plane(-d)).wait_recv()
        dqsum = dqsum + dqr[d].astype(F32)
    dqsum = (dqsum * INV).astype(BF)
    dqf[:, 0:128] = dqsum[0:128]
    dqf[:, 128:256] = dqsum[128:256]
    gx = [
        rc(dqf, dqx.at[i], x_s.at[i], x_r.at[i], dev)
        for i, dev in enumerate((mate, side, side_mate))
    ]
    for cp in (gx[1], gx[2], gx[0]):
        cp.start()

    pair.wait_recv()
    for d in range(8):
        at = pl.ds(d * 128, 128)
        zs[d] = (jnp.where(first_core, dk[at, :], dv[at, :]) + pair_r[at, :].astype(F32)).astype(BF)
    gz = {d: rc(zs.at[d], zr.at[d], z_s.at[d], z_r.at[d], ring(-d)) for d in ORDER}
    for d in ORDER:
        gz[d].start()

    for cp in wpush:
        cp.wait_recv()
    for cp in own[4:]:
        cp.wait()
    gx[1].wait_recv()
    gx[2].wait_recv()
    side_dq = jnp.concatenate([dqx[1], dqx[2]], axis=1)

    def send_part(n, carry):
        col = pl.multiple_of(4096 + n * 512, 512)
        part_s[n] = mm(side_dq, W[:, pl.ds(col, 512)]).astype(BF)
        rc(part_s.at[n], part_r.at[n], pt_s.at[n], pt_r.at[n], cross).start()
        return carry

    lax.fori_loop(0, 8, send_part, 0)

    ksum = zs[0].astype(F32)
    for d in range(1, 8):
        gz[d].wait_recv()
        ksum = ksum + zr[d].astype(F32)
    hs[...] = ksum.astype(BF)
    gh = [
        rc(hs, hr.at[i], h_s.at[i], h_r.at[i], dev)
        for i, dev in enumerate((mate, far, far_mate))
    ]
    for cp in gh:
        cp.start()
    for cp in gh:
        cp.wait_recv()
    mine = hs[...].astype(F32) + hr[1].astype(F32)
    others = hr[0].astype(F32) + hr[2].astype(F32)
    dk_all = (jnp.where(first_core, mine, others) * INV).astype(BF)
    dv_all = jnp.where(first_core, others, mine).astype(BF)
    kvg = jnp.concatenate([dk_all, dv_all], axis=1)

    gx[0].wait_recv()
    own_dq = jnp.concatenate([dqf[...], dqx[0]], axis=1)

    def finish(n, carry):
        col = pl.multiple_of(n * 512, 512)
        acc = mm(own_dq, W[:, pl.ds(col, 512)]) + mm(kvg, WK[:, pl.ds(col, 512)])
        rc(part_s.at[n], part_r.at[n], pt_s.at[n], pt_r.at[n], cross).wait_recv()
        out[:, pl.ds(col, 512)] = (acc + part_r[n].astype(F32)).astype(BF)
        return carry

    lax.fori_loop(0, 8, finish, 0)

    for d in ORDER:
        for g in (gk, gv, gmk, gq, gd, gmq, gs, gz):
            g[d].wait_send()
        rc(dqs.at[d], dqr.at[d], dq_s.at[d], dq_r.at[d], plane(-d)).wait_send()
    for cp in wpush + gx + gh + [pair]:
        cp.wait_send()
    for n in range(8):
        rc(part_s.at[n], part_r.at[n], pt_s.at[n], pt_r.at[n], cross).wait_send()


def on_device(queries, keys, values, dout, positions, doc_ids, w_query, w_kv):
    anys = pl.BlockSpec(memory_space=pl.ANY)
    smem = pl.BlockSpec(memory_space=pltpu.SMEM)
    V = pltpu.VMEM
    dma = pltpu.SemaphoreType.DMA
    scratch = [
        V((8, 128, 256), BF), V((8, 128, 256), BF), V((1024, 256), BF), V((1024, 128), BF),
        V((128, 1024), BF), V((8, 8, 128), F32), V((8, 8, 128), F32), V((8, 128), F32),
        V((128, 256), F32), V((8, 1024, 256), F32), V((8, 1024, 256), F32),
        V((2, 8, 256), F32), V((8, 256), F32), V((8, 2, 8, 256), F32), V((2, 8, 256), F32),
        V((1024, 128), F32), V((1024, 128), F32), V((8, 256, 128), BF), V((8, 256, 128), BF),
        V((1024, 128), BF), V((1024, 128), BF), V((8, 128, 128), BF), V((8, 128, 128), BF),
        V((128, 128), BF), V((3, 128, 128), BF), V((128, 256), BF), V((3, 128, 256), BF),
        V((512, 8192), BF), V((256, 4096), BF), V((8, 128, 512), BF), V((8, 128, 512), BF),
    ]
    scratch += [dma((8,))] * 18
    scratch += [dma, dma, dma((3,)), dma((3,)), dma((3,)), dma((3,)), dma((2,)), dma((2,))]
    scratch += [dma((8,)), dma((8,)), dma((7,))]
    return pl.pallas_call(
        kernel,
        out_shape=jax.ShapeDtypeStruct((128, 4096), BF),
        in_specs=[smem, smem] + [anys] * 6,
        out_specs=pl.BlockSpec(memory_space=pltpu.VMEM),
        scratch_shapes=scratch,
        compiler_params=pltpu.CompilerParams(
            collective_id=0, has_side_effects=True, vmem_limit_bytes=60 * 1024 * 1024
        ),
    )(positions, doc_ids, queries, dout, keys, values, w_query, w_kv)


def solution(mesh):
    torus = Mesh(mesh.devices.reshape(8, 2, 4, 2, 2), CTX + HEAD)
    return jax.shard_map(
        on_device,
        mesh=torus,
        in_specs=(
            P(CTX, HEAD),
            P(CTX, None),
            P(CTX, None),
            P(CTX, HEAD),
            P(CTX),
            P(CTX),
            P(HEAD, None),
            P(None, HEAD),
        ),
        out_specs=P(CTX, HEAD),
        check_vma=False,
    )
```

time: 715 us -> 81.2 us (0.11)
  blocking collectives: 257 us -> 0 us
  waiting for transfers between devices: 237 us -> 0 us
  matrix products: 110 us -> 0 us
  Pallas kernels: 0 us -> 78.8 us
  local copies, waits for them, and re-layouts: 55 us -> 2.29 us
  loops' own time: 23 us -> 0 us
  between operations: 13.3 us -> 0.01 us
  other arithmetic: 12.1 us -> 0 us
    all_gather x2 -> x0, blocking collectives: 257 us -> none  [the longest x1 133 us: on_device(): lax.all_gather(doc_ids, CTX, axis=0, tiled=True)]
    reduce_scatter x4 -> x0, waiting for transfers between devices: 228 us -> none  [the longest x3 181 us: reduced_to_own(): parts = lax.psum_scatter(parts, axes[k], scatter_dimension=0, tiled=True)]
    dot_general x114 -> x0, matrix products: 110 us -> none  [the longest x32 37.1 us: block_scores(): jnp.einsum('qhd,kd->hqk', query_rows, key_piece, preferred_element_type=j...]
    pallas_call x0 -> x1, Pallas kernels: none -> 78.8 us  [on_device(): pl.pallas_call(kernel, out_shape=jax.ShapeDtypeStruct((128, 4096), BF), i...]
    dynamic_slice x96 -> x0, local copies, waits for them, and re-layouts: 23.6 us -> none  [the longest x32 18.7 us: on_device(): totals, unused = lax.scan(forward_block, initial, numbers)]
    another operation x2 -> x0, loops' own time: 23 us -> none  [the longest x1 11.6 us: on_device(): lax.scan(backward_block, jnp.zeros((tok_rows, local_heads, head_size), jn...]
    dynamic_update_slice x32 -> x0, local copies, waits for them, and re-layouts: 16.6 us -> none  [on_device(): lax.scan(backward_block, jnp.zeros((tok_rows, local_heads, head_size), jn...]
    transpose x1 -> x0, local copies, waits for them, and re-layouts: 7.59 us -> none  [reduced_to_own(): parts = jnp.moveaxis(parts, turns, range(len(axes))).reshape(-1, *inside)]
  transfers between devices with their start and end apart: 6 -> 0, of which waited for: 6 -> 0; matrix products, arithmetic and copies ran while one was open for 1% -> 0% of each run, Pallas kernels for 0% -> 0%
where the time goes in v1:
time: 81.2 us; the launch traced here: 81.1 us
  Pallas kernels  78.8 us (97%)
  local copies, waits for them, and re-layouts  2.29 us (3%)
    pallas_call x1, Pallas kernels, on_device(): pl.pallas_call(kernel, out_shape=jax.ShapeDtypeStruct((128, 4096), BF), i...  78.8 us
    unnamed x1, local copies, waits for them, and re-layouts  2.29 us

profile of v1, /device:TPU:1, one launch (start us, length us, event | category | flops | bytes accessed | tf_op | source)
XLA Modules:
  0.0 81.1 jit_solution(12345030980815478044)
XLA Ops:
  0.0 78.8 %shard_map.82 = bf16[128,4096]{1,0:T(8,128)(2,1)} custom-call(s32[128]{0:T(128)} %pos.1, s32[128]{0:T(128)} %doc.1, bf16[128,256]{1,0:T(8,128)(2,1)} %q.1, bf16[128,256]{1,0:T(8,128)(2,1)} %do.1, bf16[128,128]{1,0:T(8,128)(2,1)} %k.1, bf16[128,128]{1,0:T(8,128)(2,1)} %v.1, bf16[256,16384]{1,0:T(8,128)(2,1)} %wq.1, bf16[256,4096]{1,0:T(8,128)(2,1)} %wkv.1), custom_call_target="tpu_custom_call" | custom-call | tf_op jit(solution)/shard_map/pallas_call | solution.py:334
  78.8 2.3 %copy.10 = bf16[128,4096]{1,0:T(8,128)(2,1)} copy(bf16[128,4096]{1,0:T(8,128)(2,1)} %shard_map.82) | data formatting | bytes 2097152

commit v2 on v1

--- a/solution.py
+++ b/solution.py
@@ -1,3 +1,4 @@
+import functools
 import math
 
 import jax
@@ -27,9 +28,9 @@
 def kernel(
     pos, doc, q, do, k, v, wq, wkv, out,
     Q, DO, KA, V, KT, MQ, MK, meta, tri, S, DP, stat, mloc, stat_all, coef,
-    dk, dv, dqs, dqr, pair_s, pair_r, zs, zr, hs, hr, dqf, dqx, W, WK, part_s, part_r,
+    dk, dv, dqs, dqr, pair_s, pair_r, zs, zr, hs, hr, dqf, dqx, W, WK, acc,
     q_s, q_r, d_s, d_r, k_s, k_r, v_s, v_r, mq_s, mq_r, mk_s, mk_r, st_s, st_r,
-    dq_s, dq_r, z_s, z_r, pr_s, pr_r, h_s, h_r, x_s, x_r, w_s, w_r, pt_s, pt_r, loc,
+    dq_s, dq_r, z_s, z_r, pr_s, pr_r, h_s, h_r, x_s, x_r, w_s, w_r, cs, cr, fs, fr, loc,
 ):
     z, yl, x = lax.axis_index("z"), lax.axis_index("yl"), lax.axis_index("x")
     u, c = lax.axis_index("u"), lax.axis_index("c")
@@ -44,10 +45,11 @@
 
     mate = (z, yl, x, u, 1 - c)
     side = (z, 1 - yl, x, u, c)
-    side_mate = (z, 1 - yl, x, u, 1 - c)
+    left, right = (z, yl, (x + 3) % 4, u, c), (z, yl, (x + 1) % 4, u, c)
     far = (z, yl, x, 1 - u, c)
     far_mate = (z, yl, x, 1 - u, 1 - c)
     cross = (z, 1 - yl, x, 1 - u, c)
+    cross_mate = (z, 1 - yl, x, 1 - u, 1 - c)
 
     def rc(src, dst, ss, rs, dev):
         return pltpu.make_async_remote_copy(
@@ -62,11 +64,8 @@
         pltpu.make_async_copy(do, DO.at[0], loc.at[1]),
         pltpu.make_async_copy(k, KA.at[pl.ds(0, 128), pl.ds(0, 128)], loc.at[2]),
         pltpu.make_async_copy(v, V.at[pl.ds(0, 128)], loc.at[3]),
-        pltpu.make_async_copy(wq.at[:, cols(u, c)], W.at[pl.ds(0, 256), pl.ds(0, 4096)], loc.at[4]),
-        pltpu.make_async_copy(
-            wq.at[:, cols(1 - u, c)], W.at[pl.ds(0, 256), pl.ds(4096, 4096)], loc.at[5]
-        ),
-        pltpu.make_async_copy(wkv, WK, loc.at[6]),
+        pltpu.make_async_copy(wq.at[:, cols(u, c)], W.at[pl.ds(0, 256)], loc.at[4]),
+        pltpu.make_async_copy(wkv, WK, loc.at[5]),
     ]
 
     lane = lax.broadcasted_iota(jnp.int32, (1, 128), 1)
@@ -89,7 +88,7 @@
 
     barrier = pltpu.get_barrier_semaphore()
     peers = [plane(d) for d in range(1, 8)] + [ring(d) for d in range(1, 8)]
-    peers += [mate, side_mate, far, far_mate, cross]
+    peers += [mate, far, far_mate, cross, cross_mate]
     for dev in peers:
         pl.semaphore_signal(barrier, inc=1, device_id=dev, device_id_type=MESH)
     for cp in own[:4]:
@@ -110,10 +109,49 @@
         gmq[d].start()
         gq[d].start()
         gd[d].start()
-    wpush = [
-        rc(wq.at[:, cols(u, 1 - c)], W.at[pl.ds(256, 256), pl.ds(0, 4096)], w_s.at[0], w_r.at[0], mate),
-        rc(wq.at[:, cols(1 - u, 1 - c)], W.at[pl.ds(256, 256), pl.ds(4096, 4096)], w_s.at[1], w_r.at[1], mate),
-    ]
+    def colors(yy):
+        return ((x + 2 * yy) % 4, (z + 2 * yy) % 4, (x + 2 * z) % 4, (z + 2 * x) % 4)
+
+    def sub(part, color, base=0):
+        return pl.ds(pl.multiple_of(base + part * 1024 + color * 256, 256), 256)
+
+    mine_c, theirs_c = colors(yl), colors(1 - yl)
+    over = []
+    for f in range(4):
+        at = [(2 * (1 - u) + cc) * 4096 for cc in (c, 1 - c)]
+        into = sub(f, theirs_c[f])
+        over.append((
+            rc(wq.at[:, sub(f, theirs_c[f], at[0])], W.at[pl.ds(512, 256), into], cs.at[f, 0], cr.at[f, 0], cross),
+            rc(wq.at[:, sub(f, theirs_c[f], at[1])], W.at[pl.ds(768, 256), into], cs.at[f, 1], cr.at[f, 1], cross_mate),
+        ))
+    for pair_of in over:
+        for cp in pair_of:
+            cp.start()
+
+    whole, upper, lower = pl.ds(512, 512), pl.ds(512, 256), pl.ds(768, 256)
+    xs = [(right, whole), (left, whole)]
+    zz = [(ring(1), whole), (ring(-1), whole)]
+    routes = (
+        xs + [(side, whole)],
+        zz + [(side, whole)],
+        xs + [(ring(1), upper), (ring(-1), lower)],
+        zz + [(right, upper), (left, lower)],
+    )
+    relays = []
+    for f in range(4):
+        at = sub(f, mine_c[f])
+        relays.append([
+            rc(W.at[part, at], W.at[part, at], fs.at[f, i], fr.at[f, i], dev)
+            for i, (dev, part) in enumerate(routes[f])
+        ])
+
+    def relay(f):
+        for cp in over[f]:
+            cp.wait_recv()
+        for cp in relays[f]:
+            cp.start()
+
+    wpush = [rc(wq.at[:, cols(u, 1 - c)], W.at[pl.ds(256, 256)], w_s, w_r, mate)]
     for cp in wpush:
         cp.start()
     for cp in own[4:]:
@@ -141,7 +179,13 @@
     def fold(val, op):
         return op(val.reshape(32, 8, 256), axis=0)
 
-    def first(d, carry):
+    def slot(g, j):
+        owner = g * 4 + (x - j + 4) % 4
+        return owner, (p - owner + 8) % 8
+
+    def first(g, j, carry):
+        owner, d = slot(g, j)
+
         @pl.when(d > 0)
         def _():
             rc(meta, MQ.at[d], mq_s.at[d], mq_r.at[d], plane(d)).wait_recv()
@@ -175,40 +219,46 @@
             mixed = mixed + fold(e * DP[d, at, :], jnp.sum)
         total = jnp.sum(total, axis=0, keepdims=True)
         mixed = jnp.sum(mixed, axis=0, keepdims=True)
-        mloc[pl.ds(d, 1), :] = m * INV
-        stat[0, pl.ds(d, 1), :] = m * INV + jnp.log(total)
-        stat[1, pl.ds(d, 1), :] = mixed / total
+        mloc[g, pl.ds(owner - g * 4, 1), :] = m * INV
+        stat[g, pl.ds(owner - g * 4, 1), :] = m * INV + jnp.log(total)
+        stat[g, pl.ds(owner - g * 4 + 4, 1), :] = mixed / total
         return carry
 
-    lax.fori_loop(0, 8, first, 0)
-
-    gs = {d: rc(stat, stat_all.at[d], st_s.at[d], st_r.at[d], plane(d)) for d in ORDER}
-    for d in ORDER:
-        gs[d].start()
-    lses, deltas = [stat[0]], [stat[1]]
-    for d in range(1, 8):
-        gs[d].wait_recv()
-        for row, into in ((0, lses), (1, deltas)):
-            a = stat_all[d, row]
-            into.append(jnp.concatenate([a[8 - d :], a[: 8 - d]], axis=0))
-    big = lses[0]
-    for a in lses[1:]:
-        big = jnp.maximum(big, a)
-    tot = jnp.zeros((8, 256), F32)
-    mix = jnp.zeros((8, 256), F32)
-    for a, b in zip(lses, deltas):
-        w = jnp.exp(a - big)
-        tot = tot + w
-        mix = mix + w * b
-    coef[0] = jnp.exp(mloc[...] - (big + jnp.log(tot)))
-    coef[1] = mix / tot
+    gs = [
+        {d: rc(stat.at[g], stat_all.at[d, g], st_s.at[d, g], st_r.at[d, g], plane(d)) for d in ORDER}
+        for g in range(2)
+    ]
+    relay(0)
+    for g in range(2):
+        lax.fori_loop(0, 4, functools.partial(first, g), 0)
+        for d in ORDER:
+            gs[g][d].start()
+        relay(1 + g)
+
+    def merge(g):
+        parts = [stat[g]]
+        for d in range(1, 8):
+            gs[g][d].wait_recv()
+            parts.append(stat_all[d, g])
+        big = parts[0][0:4]
+        for a in parts[1:]:
+            big = jnp.maximum(big, a[0:4])
+        tot = jnp.zeros((4, 256), F32)
+        mix = jnp.zeros((4, 256), F32)
+        for a in parts:
+            w = jnp.exp(a[0:4] - big)
+            tot = tot + w
+            mix = mix + w * a[4:8]
+        coef[g, 0:4, :] = jnp.exp(mloc[g] - (big + jnp.log(tot)))
+        coef[g, 4:8, :] = mix / tot
 
     dk[...] = jnp.zeros_like(dk)
     dv[...] = jnp.zeros_like(dv)
 
-    def second(d, carry):
-        f = coef[0, pl.ds(d, 1), :]
-        delta = coef[1, pl.ds(d, 1), :]
+    def second(g, j, carry):
+        owner, d = slot(g, j)
+        f = coef[g, pl.ds(owner - g * 4, 1), :]
+        delta = coef[g, pl.ds(owner - g * 4 + 4, 1), :]
         qq = stacked(Q, d)
         dd = stacked(DO, d)
         dqt = jnp.zeros((128, 256), F32)
@@ -227,7 +277,11 @@
 
         return carry
 
-    lax.fori_loop(0, 8, second, 0)
+    for g in range(2):
+        merge(g)
+        lax.fori_loop(0, 4, functools.partial(second, g), 0)
+        if g == 0:
+            relay(3)
 
     first_core = c == 0
     pair_s[...] = jnp.where(first_core, dv[...], dk[...]).astype(BF)
@@ -243,9 +297,9 @@
     dqf[:, 128:256] = dqsum[128:256]
     gx = [
         rc(dqf, dqx.at[i], x_s.at[i], x_r.at[i], dev)
-        for i, dev in enumerate((mate, side, side_mate))
-    ]
-    for cp in (gx[1], gx[2], gx[0]):
+        for i, dev in enumerate((mate, far, far_mate))
+    ]
+    for cp in (gx[2], gx[1], gx[0]):
         cp.start()
 
     pair.wait_recv()
@@ -260,17 +314,19 @@
         cp.wait_recv()
     for cp in own[4:]:
         cp.wait()
-    gx[1].wait_recv()
-    gx[2].wait_recv()
-    side_dq = jnp.concatenate([dqx[1], dqx[2]], axis=1)
-
-    def send_part(n, carry):
-        col = pl.multiple_of(4096 + n * 512, 512)
-        part_s[n] = mm(side_dq, W[:, pl.ds(col, 512)]).astype(BF)
-        rc(part_s.at[n], part_r.at[n], pt_s.at[n], pt_r.at[n], cross).start()
+    for group in relays:
+        for cp in group:
+            cp.wait_recv()
+    for cp in gx:
+        cp.wait_recv()
+    all_dq = jnp.concatenate([dqf[...], dqx[0], dqx[1], dqx[2]], axis=1)
+
+    def query_part(n, carry):
+        col = pl.ds(pl.multiple_of(n * 512, 512), 512)
+        acc[:, col] = mm(all_dq, W[:, col])
         return carry
 
-    lax.fori_loop(0, 8, send_part, 0)
+    lax.fori_loop(0, 8, query_part, 0)
 
     ksum = zs[0].astype(F32)
     for d in range(1, 8):
@@ -291,26 +347,22 @@
     dv_all = jnp.where(first_core, others, mine).astype(BF)
     kvg = jnp.concatenate([dk_all, dv_all], axis=1)
 
-    gx[0].wait_recv()
-    own_dq = jnp.concatenate([dqf[...], dqx[0]], axis=1)
-
     def finish(n, carry):
-        col = pl.multiple_of(n * 512, 512)
-        acc = mm(own_dq, W[:, pl.ds(col, 512)]) + mm(kvg, WK[:, pl.ds(col, 512)])
-        rc(part_s.at[n], part_r.at[n], pt_s.at[n], pt_r.at[n], cross).wait_recv()
-        out[:, pl.ds(col, 512)] = (acc + part_r[n].astype(F32)).astype(BF)
+        col = pl.ds(pl.multiple_of(n * 512, 512), 512)
+        out[:, col] = (acc[:, col] + mm(kvg, WK[:, col])).astype(BF)
         return carry
 
     lax.fori_loop(0, 8, finish, 0)
 
     for d in ORDER:
-        for g in (gk, gv, gmk, gq, gd, gmq, gs, gz):
+        for g in (gk, gv, gmk, gq, gd, gmq, gs[0], gs[1], gz):
             g[d].wait_send()
         rc(dqs.at[d], dqr.at[d], dq_s.at[d], dq_r.at[d], plane(-d)).wait_send()
     for cp in wpush + gx + gh + [pair]:
         cp.wait_send()
-    for n in range(8):
-        rc(part_s.at[n], part_r.at[n], pt_s.at[n], pt_r.at[n], cross).wait_send()
+    for f in range(4):
+        for cp in relays[f] + list(over[f]):
+            cp.wait_send()
 
 
 def on_device(queries, keys, values, dout, positions, doc_ids, w_query, w_kv):
@@ -322,15 +374,15 @@
         V((8, 128, 256), BF), V((8, 128, 256), BF), V((1024, 256), BF), V((1024, 128), BF),
         V((128, 1024), BF), V((8, 8, 128), F32), V((8, 8, 128), F32), V((8, 128), F32),
         V((128, 256), F32), V((8, 1024, 256), F32), V((8, 1024, 256), F32),
-        V((2, 8, 256), F32), V((8, 256), F32), V((8, 2, 8, 256), F32), V((2, 8, 256), F32),
+        V((2, 8, 256), F32), V((2, 4, 256), F32), V((8, 2, 8, 256), F32), V((2, 8, 256), F32),
         V((1024, 128), F32), V((1024, 128), F32), V((8, 256, 128), BF), V((8, 256, 128), BF),
         V((1024, 128), BF), V((1024, 128), BF), V((8, 128, 128), BF), V((8, 128, 128), BF),
         V((128, 128), BF), V((3, 128, 128), BF), V((128, 256), BF), V((3, 128, 256), BF),
-        V((512, 8192), BF), V((256, 4096), BF), V((8, 128, 512), BF), V((8, 128, 512), BF),
-    ]
-    scratch += [dma((8,))] * 18
-    scratch += [dma, dma, dma((3,)), dma((3,)), dma((3,)), dma((3,)), dma((2,)), dma((2,))]
-    scratch += [dma((8,)), dma((8,)), dma((7,))]
+        V((1024, 4096), BF), V((256, 4096), BF), V((128, 4096), F32),
+    ]
+    scratch += [dma((8,))] * 12 + [dma((8, 2))] * 2 + [dma((8,))] * 4
+    scratch += [dma, dma, dma((3,)), dma((3,)), dma((3,)), dma((3,)), dma, dma]
+    scratch += [dma((4, 2)), dma((4, 2)), dma((4, 4)), dma((4, 4)), dma((6,))]
     return pl.pallas_call(
         kernel,
         out_shape=jax.ShapeDtypeStruct((128, 4096), BF),

time: 81.2 us -> 68.9 us (0.85)
  the two profiles are of different devices: /device:TPU:1 before, /device:TPU:41 now
where the time goes in v2:
time: 68.9 us; the launch traced here: 68.7 us
  Pallas kernels  66.4 us (96%)
  local copies, waits for them, and re-layouts  2.29 us (3%)
    pallas_call x1, Pallas kernels, on_device(): pl.pallas_call(kernel, out_shape=jax.ShapeDtypeStruct((128, 4096), BF), i...  66.4 us
    unnamed x1, local copies, waits for them, and re-layouts  2.29 us

profile of v2, /device:TPU:41, one launch (start us, length us, event | category | flops | bytes accessed | tf_op | source)
XLA Modules:
  0.0 68.7 jit_solution(15576882553368139139)
XLA Ops:
  0.0 66.4 %shard_map.82 = bf16[128,4096]{1,0:T(8,128)(2,1)} custom-call(s32[128]{0:T(128)} %pos.1, s32[128]{0:T(128)} %doc.1, bf16[128,256]{1,0:T(8,128)(2,1)} %q.1, bf16[128,256]{1,0:T(8,128)(2,1)} %do.1, bf16[128,128]{1,0:T(8,128)(2,1)} %k.1, bf16[128,128]{1,0:T(8,128)(2,1)} %v.1, bf16[256,16384]{1,0:T(8,128)(2,1)} %wq.1, bf16[256,4096]{1,0:T(8,128)(2,1)} %wkv.1), custom_call_target="tpu_custom_call" | custom-call | tf_op jit(solution)/shard_map/pallas_call | solution.py:386
  66.5 2.3 %copy.10 = bf16[128,4096]{1,0:T(8,128)(2,1)} copy(bf16[128,4096]{1,0:T(8,128)(2,1)} %shard_map.82) | data formatting | bytes 2097152

commit v3 on v2

--- a/solution.py
+++ b/solution.py
@@ -27,18 +27,19 @@
 
 def kernel(
     pos, doc, q, do, k, v, wq, wkv, out,
-    Q, DO, KA, V, KT, MQ, MK, meta, tri, S, DP, stat, mloc, stat_all, coef,
+    QD, KV, OH, KT, MQ, MK, meta, tri, S, DP, stat, mloc, stat_all, coef,
     dk, dv, dqs, dqr, pair_s, pair_r, zs, zr, hs, hr, dqf, dqx, W, WK, acc,
     q_s, q_r, d_s, d_r, k_s, k_r, v_s, v_r, mq_s, mq_r, mk_s, mk_r, st_s, st_r,
     dq_s, dq_r, z_s, z_r, pr_s, pr_r, h_s, h_r, x_s, x_r, w_s, w_r, cs, cr, fs, fr, loc,
 ):
     z, yl, x = lax.axis_index("z"), lax.axis_index("yl"), lax.axis_index("x")
     u, c = lax.axis_index("u"), lax.axis_index("c")
-    p = yl * 4 + x
 
     def plane(d):
-        t = (p + d + 8) % 8
-        return (z, t // 4, t % 4, u, c)
+        return (z, (yl + d // 4) % 2, (x + d % 4) % 4, u, c)
+
+    def owner_of(d):
+        return (z, (yl + d // 4) % 2, (x + 4 - d % 4) % 4, u, c)
 
     def ring(d):
         return ((z + d + 8) % 8, yl, x, u, c)
@@ -60,10 +61,10 @@
         return pl.ds(pl.multiple_of((2 * uu + cc) * 4096, 4096), 4096)
 
     own = [
-        pltpu.make_async_copy(q, Q.at[0], loc.at[0]),
-        pltpu.make_async_copy(do, DO.at[0], loc.at[1]),
-        pltpu.make_async_copy(k, KA.at[pl.ds(0, 128), pl.ds(0, 128)], loc.at[2]),
-        pltpu.make_async_copy(v, V.at[pl.ds(0, 128)], loc.at[3]),
+        pltpu.make_async_copy(q, QD.at[0, 0], loc.at[0]),
+        pltpu.make_async_copy(do, QD.at[0, 1], loc.at[1]),
+        pltpu.make_async_copy(k, KV.at[0, 0], loc.at[2]),
+        pltpu.make_async_copy(v, KV.at[1, 0], loc.at[3]),
         pltpu.make_async_copy(wq.at[:, cols(u, c)], W.at[pl.ds(0, 256)], loc.at[4]),
         pltpu.make_async_copy(wkv, WK, loc.at[5]),
     ]
@@ -96,19 +97,42 @@
     pl.semaphore_wait(barrier, len(peers))
 
     ORDER = (1, 7, 2, 6, 3, 5, 4)
-    gk = {d: rc(k, KA.at[pl.ds(d * 128, 128), pl.ds(0, 128)], k_s.at[d], k_r.at[d], ring(d)) for d in ORDER}
-    gv = {d: rc(v, V.at[pl.ds(d * 128, 128)], v_s.at[d], v_r.at[d], ring(d)) for d in ORDER}
+    gk = {d: rc(k, KV.at[c, d], k_s.at[d], k_r.at[d], ring(d)) for d in ORDER}
+    gv = {d: rc(v, KV.at[c, d], k_s.at[d], k_r.at[d], ring(d)) for d in ORDER}
+    gkv = {d: rc(KV.at[c, d], KV.at[c, d], v_s.at[d], v_r.at[d], mate) for d in ORDER}
     gmk = {d: rc(meta, MK.at[d], mk_s.at[d], mk_r.at[d], ring(d)) for d in ORDER}
-    gq = {d: rc(q, Q.at[d], q_s.at[d], q_r.at[d], plane(d)) for d in ORDER}
-    gd = {d: rc(do, DO.at[d], d_s.at[d], d_r.at[d], plane(d)) for d in ORDER}
     gmq = {d: rc(meta, MQ.at[d], mq_s.at[d], mq_r.at[d], plane(d)) for d in ORDER}
+
+    def qd(i, src, d, dev):
+        sems = (q_s, q_r) if i == 0 else (d_s, d_r)
+        return rc(src, QD.at[d, i], sems[0].at[d], sems[1].at[d], dev)
+
+    gq = {
+        1: (qd(0, q, 1, right), qd(1, do, 1, right)),
+        3: (qd(0, q, 3, left), qd(1, do, 3, left)),
+        4: (qd(0, q, 4, side), qd(1, do, 4, side)),
+        2: (qd(0, QD.at[1, 0], 2, right), qd(1, QD.at[3, 1], 2, left)),
+        5: (qd(0, QD.at[4, 0], 5, right), qd(1, QD.at[4, 1], 5, right)),
+        7: (qd(0, QD.at[4, 0], 7, left), qd(1, QD.at[4, 1], 7, left)),
+        6: (qd(0, QD.at[2, 0], 6, side), qd(1, QD.at[2, 1], 6, side)),
+    }
+
+    @pl.when(c == 0)
+    def _():
+        for d in ORDER:
+            gk[d].start()
+
+    @pl.when(c == 1)
+    def _():
+        for d in ORDER:
+            gv[d].start()
+
+    for d, i in ((1, 0), (3, 1), (4, 0), (1, 1), (3, 0), (4, 1)):
+        gq[d][i].start()
     for d in ORDER:
         gmk[d].start()
-        gk[d].start()
-        gv[d].start()
         gmq[d].start()
-        gq[d].start()
-        gd[d].start()
+
     def colors(yy):
         return ((x + 2 * yy) % 4, (z + 2 * yy) % 4, (x + 2 * z) % 4, (z + 2 * x) % 4)
 
@@ -162,51 +186,77 @@
         b = jnp.broadcast_to(ref[d, row + 1 : row + 2, :], (64, 128))
         return jnp.concatenate([a, b], axis=0).astype(BF)
 
+    def pass_on(*which):
+        for d in which:
+            gk[d].wait_recv()
+            gkv[d].start()
+
+    pass_on(1, 7)
+    gq[1][0].wait_recv()
+    gq[2][0].start()
+    gq[3][1].wait_recv()
+    gq[2][1].start()
+    gq[4][0].wait_recv()
+    gq[5][0].start()
+    gq[7][0].start()
+    pass_on(2, 6)
+    gq[4][1].wait_recv()
+    gq[5][1].start()
+    gq[7][1].start()
+    gq[1][1].wait_recv()
+    gq[3][0].wait_recv()
+    pass_on(3, 5)
+    for i in range(2):
+        gq[2][i].wait_recv()
+        gq[6][i].start()
+    pass_on(4)
     for cp in own[:4]:
         cp.wait()
-    for d in range(8):
+    for d in (0,) + ORDER:
         if d:
             gmk[d].wait_recv()
-            gk[d].wait_recv()
-            gv[d].wait_recv()
+            gkv[d].wait_recv()
         at = pl.ds(d * 128, 128)
-        KA[at, 128:256] = runs(MK, d, 2)
-        KT[:, d * 128 : (d + 1) * 128] = KA[at, 0:128].astype(F32).T.astype(BF)
-
-    def stacked(ref, d):
-        return jnp.concatenate([ref[d, :, 0:128], ref[d, :, 128:256]], axis=0)
+        OH[at, :] = runs(MK, d, 2)
+        KT[:, d * 128 : (d + 1) * 128] = KV[0, d].astype(F32).T.astype(BF)
+    for d in ORDER:
+        gmq[d].wait_recv()
+
+    def rows_of(i, n):
+        return KV[i, 2 * n : 2 * n + 2].reshape(256, 128)
+
+    def stacked(i, d):
+        return jnp.concatenate([QD[d, i, :, 0:128], QD[d, i, :, 128:256]], axis=0)
 
     def fold(val, op):
         return op(val.reshape(32, 8, 256), axis=0)
 
-    def slot(g, j):
-        owner = g * 4 + (x - j + 4) % 4
-        return owner, (p - owner + 8) % 8
+    def slot(g, dx):
+        return (x - dx + 4) % 4, ((yl + g) % 2) * 4 + dx
 
     def first(g, j, carry):
-        owner, d = slot(g, j)
-
-        @pl.when(d > 0)
+        owner, d = slot(g, j + (j // 2) * (5 - 2 * j))
+
+        @pl.when(d >= 5)
         def _():
-            rc(meta, MQ.at[d], mq_s.at[d], mq_r.at[d], plane(d)).wait_recv()
-            rc(q, Q.at[d], q_s.at[d], q_r.at[d], plane(d)).wait_recv()
-            rc(do, DO.at[d], d_s.at[d], d_r.at[d], plane(d)).wait_recv()
+            qd(0, q, d, right).wait_recv()
+            qd(1, do, d, right).wait_recv()
 
         bias = runs(MQ, d, 0)
         qa = jnp.concatenate(
-            [stacked(Q, d), jnp.concatenate([bias, bias], axis=0)], axis=1
+            [stacked(0, d), jnp.concatenate([bias, bias], axis=0)], axis=1
         )
-        dd = stacked(DO, d)
+        dd = stacked(1, d)
         own_tile = jnp.where(d == 0, 1.0, 0.0)
         top = jnp.full((8, 256), -3e38, F32)
         for n in range(4):
             at = pl.ds(n * 256, 256)
-            s = mm(KA[at, :], qa, NT)
+            s = mm(jnp.concatenate([rows_of(0, n), OH[at, :]], axis=1), qa, NT)
             if n == 0:
                 s = jnp.concatenate([s[0:128] + tri[...] * own_tile, s[128:256]], axis=0)
             S[d, at, :] = s
             top = jnp.maximum(top, fold(s, jnp.max))
-            DP[d, at, :] = mm(V[at, :], dd, NT)
+            DP[d, at, :] = mm(rows_of(1, n), dd, NT)
         m = jnp.max(top, axis=0, keepdims=True)
         mc = m * (INV * LOG2E)
         total = jnp.zeros((8, 256), F32)
@@ -219,9 +269,9 @@
             mixed = mixed + fold(e * DP[d, at, :], jnp.sum)
         total = jnp.sum(total, axis=0, keepdims=True)
         mixed = jnp.sum(mixed, axis=0, keepdims=True)
-        mloc[g, pl.ds(owner - g * 4, 1), :] = m * INV
-        stat[g, pl.ds(owner - g * 4, 1), :] = m * INV + jnp.log(total)
-        stat[g, pl.ds(owner - g * 4 + 4, 1), :] = mixed / total
+        mloc[g, pl.ds(owner, 1), :] = m * INV
+        stat[g, pl.ds(owner, 1), :] = m * INV + jnp.log(total)
+        stat[g, pl.ds(owner + 4, 1), :] = mixed / total
         return carry
 
     gs = [
@@ -256,11 +306,11 @@
     dv[...] = jnp.zeros_like(dv)
 
     def second(g, j, carry):
-        owner, d = slot(g, j)
-        f = coef[g, pl.ds(owner - g * 4, 1), :]
-        delta = coef[g, pl.ds(owner - g * 4 + 4, 1), :]
-        qq = stacked(Q, d)
-        dd = stacked(DO, d)
+        owner, d = slot(g, (2 - j) * (1 - j // 2) + (9 - 3 * j) * (j // 2))
+        f = coef[g, pl.ds(owner, 1), :]
+        delta = coef[g, pl.ds(owner + 4, 1), :]
+        qq = stacked(0, d)
+        dd = stacked(1, d)
         dqt = jnp.zeros((128, 256), F32)
         for n in range(4):
             at = pl.ds(n * 256, 256)
@@ -273,7 +323,7 @@
 
         @pl.when(d > 0)
         def _():
-            rc(dqs.at[d], dqr.at[d], dq_s.at[d], dq_r.at[d], plane(-d)).start()
+            rc(dqs.at[d], dqr.at[d], dq_s.at[d], dq_r.at[d], owner_of(d)).start()
 
         return carry
 
@@ -290,7 +340,7 @@
 
     dqsum = dqs[0].astype(F32)
     for d in range(1, 8):
-        rc(dqs.at[d], dqr.at[d], dq_s.at[d], dq_r.at[d], plane(-d)).wait_recv()
+        rc(dqs.at[d], dqr.at[d], dq_s.at[d], dq_r.at[d], owner_of(d)).wait_recv()
         dqsum = dqsum + dqr[d].astype(F32)
     dqsum = (dqsum * INV).astype(BF)
     dqf[:, 0:128] = dqsum[0:128]
@@ -355,9 +405,11 @@
     lax.fori_loop(0, 8, finish, 0)
 
     for d in ORDER:
-        for g in (gk, gv, gmk, gq, gd, gmq, gs[0], gs[1], gz):
+        for g in (gk, gkv, gmk, gmq, gs[0], gs[1], gz):
             g[d].wait_send()
-        rc(dqs.at[d], dqr.at[d], dq_s.at[d], dq_r.at[d], plane(-d)).wait_send()
+        for cp in gq[d]:
+            cp.wait_send()
+        rc(dqs.at[d], dqr.at[d], dq_s.at[d], dq_r.at[d], owner_of(d)).wait_send()
     for cp in wpush + gx + gh + [pair]:
         cp.wait_send()
     for f in range(4):
@@ -371,7 +423,7 @@
     V = pltpu.VMEM
     dma = pltpu.SemaphoreType.DMA
     scratch = [
-        V((8, 128, 256), BF), V((8, 128, 256), BF), V((1024, 256), BF), V((1024, 128), BF),
+        V((8, 2, 128, 256), BF), V((2, 8, 128, 128), BF), V((1024, 128), BF),
         V((128, 1024), BF), V((8, 8, 128), F32), V((8, 8, 128), F32), V((8, 128), F32),
         V((128, 256), F32), V((8, 1024, 256), F32), V((8, 1024, 256), F32),
         V((2, 8, 256), F32), V((2, 4, 256), F32), V((8, 2, 8, 256), F32), V((2, 8, 256), F32),
@@ -385,7 +437,7 @@
     scratch += [dma((4, 2)), dma((4, 2)), dma((4, 4)), dma((4, 4)), dma((6,))]
     return pl.pallas_call(
         kernel,
-        out_shape=jax.ShapeDtypeStruct((128, 4096), BF),
+        out_shape=pltpu.VMEM((128, 4096), BF),
         in_specs=[smem, smem] + [anys] * 6,
         out_specs=pl.BlockSpec(memory_space=pltpu.VMEM),
         scratch_shapes=scratch,

time: 68.9 us -> 63.4 us (0.920)
  the two profiles are of different devices: /device:TPU:41 before, /device:TPU:1 now
where the time goes in v3:
time: 63.4 us; the launch traced here: 62.5 us
  Pallas kernels  61.5 us (97%)
  local copies, waits for them, and re-layouts  0.97 us (2%)
    pallas_call x1, Pallas kernels, on_device(): pl.pallas_call(kernel, out_shape=pltpu.VMEM((128, 4096), BF), in_specs=[s...  61.5 us

profile of v3, /device:TPU:1, one launch (start us, length us, event | category | flops | bytes accessed | tf_op | source)
XLA Modules:
  0.0 62.5 jit_solution(1575777763017728131)
XLA Ops:
  0.0 61.5 %shard_map.82 = bf16[128,4096]{1,0:T(8,128)(2,1)S(1)} custom-call(s32[128]{0:T(128)} %pos.1, s32[128]{0:T(128)} %doc.1, bf16[128,256]{1,0:T(8,128)(2,1)} %q.1, bf16[128,256]{1,0:T(8,128)(2,1)} %do.1, bf16[128,128]{1,0:T(8,128)(2,1)} %k.1, bf16[128,128]{1,0:T(8,128)(2,1)} %v.1, bf16[256,16384]{1,0:T(8,128)(2,1)} %wq.1, bf16[256,4096]{1,0:T(8,128)(2,1)} %wkv.1), custom_call_target="tpu_custom_call" | custom-call | tf_op jit(solution)/shard_map/pallas_call | solution.py:438
  61.5 1.0 %copy.10 = bf16[128,4096]{1,0:T(8,128)(2,1)} copy(bf16[128,4096]{1,0:T(8,128)(2,1)S(1)} %shard_map.82) | data formatting | bytes 2097152

commit v4 on v3

--- a/solution.py
+++ b/solution.py
@@ -88,8 +88,7 @@
     tri[...] = jnp.where((jj // 64 == ii // 64) & (jj > ii), NEG, 0.0)
 
     barrier = pltpu.get_barrier_semaphore()
-    peers = [plane(d) for d in range(1, 8)] + [ring(d) for d in range(1, 8)]
-    peers += [mate, far, far_mate, cross, cross_mate]
+    peers = [mate, left, right, side, ring(1), ring(-1), cross, cross_mate]
     for dev in peers:
         pl.semaphore_signal(barrier, inc=1, device_id=dev, device_id_type=MESH)
     for cp in own[:4]:
@@ -97,11 +96,35 @@
     pl.semaphore_wait(barrier, len(peers))
 
     ORDER = (1, 7, 2, 6, 3, 5, 4)
-    gk = {d: rc(k, KV.at[c, d], k_s.at[d], k_r.at[d], ring(d)) for d in ORDER}
-    gv = {d: rc(v, KV.at[c, d], k_s.at[d], k_r.at[d], ring(d)) for d in ORDER}
+    up, down = ring(1), ring(-1)
+    halves = (pl.ds(0, 64), pl.ds(64, 64))
+
+    def kv_hop(src, d, dev):
+        return rc(src, KV.at[c, d], k_s.at[d], k_r.at[d], dev)
+
+    def kv_half(d, half, sem, dev):
+        part = halves[half]
+        return rc(KV.at[c, d, part], KV.at[c, 4, part], k_s.at[sem], k_r.at[sem], dev)
+
+    gk = {1: kv_hop(k, 1, up), 7: kv_hop(k, 7, down)}
+    gv = {1: kv_hop(v, 1, up), 7: kv_hop(v, 7, down)}
+    for d in (2, 3):
+        gk[d] = kv_hop(KV.at[c, d - 1], d, up)
+        gk[8 - d] = kv_hop(KV.at[c, 9 - d], 8 - d, down)
+    gk[4] = kv_half(3, 0, 4, up)
+    gk[0] = kv_half(5, 1, 0, down)
     gkv = {d: rc(KV.at[c, d], KV.at[c, d], v_s.at[d], v_r.at[d], mate) for d in ORDER}
-    gmk = {d: rc(meta, MK.at[d], mk_s.at[d], mk_r.at[d], ring(d)) for d in ORDER}
-    gmq = {d: rc(meta, MQ.at[d], mq_s.at[d], mq_r.at[d], plane(d)) for d in ORDER}
+
+    def hop(buf, sems, d, dev, src):
+        return rc(meta if src == 0 else buf.at[src], buf.at[d], sems[0].at[d], sems[1].at[d], dev)
+
+    mk = (mk_s, mk_r)
+    gmk = {d: hop(MK, mk, d, up, d - 1) for d in (1, 2, 3, 4)}
+    gmk.update({d: hop(MK, mk, d, down, (d + 1) % 8) for d in (7, 6, 5)})
+    mq = (mq_s, mq_r)
+    gmq = {1: hop(MQ, mq, 1, right, 0), 3: hop(MQ, mq, 3, left, 0), 4: hop(MQ, mq, 4, side, 0)}
+    gmq.update({2: hop(MQ, mq, 2, right, 1), 5: hop(MQ, mq, 5, right, 4)})
+    gmq.update({7: hop(MQ, mq, 7, left, 4), 6: hop(MQ, mq, 6, side, 2)})
 
     def qd(i, src, d, dev):
         sems = (q_s, q_r) if i == 0 else (d_s, d_r)
@@ -119,22 +142,23 @@
 
     @pl.when(c == 0)
     def _():
-        for d in ORDER:
-            gk[d].start()
+        gk[1].start()
+        gk[7].start()
 
     @pl.when(c == 1)
     def _():
-        for d in ORDER:
-            gv[d].start()
-
+        gv[1].start()
+        gv[7].start()
+
+    for d in (1, 7):
+        gmk[d].start()
+    for d in (1, 3, 4):
+        gmq[d].start()
     for d, i in ((1, 0), (3, 1), (4, 0), (1, 1), (3, 0), (4, 1)):
         gq[d][i].start()
-    for d in ORDER:
-        gmk[d].start()
-        gmq[d].start()
 
     def colors(yy):
-        return ((x + 2 * yy) % 4, (z + 2 * yy) % 4, (x + 2 * z) % 4, (z + 2 * x) % 4)
+        return ((x + 2 * yy) % 4, (z + 2 * x) % 4, (z + 2 * x) % 4, (z + 2 * yy) % 4)
 
     def sub(part, color, base=0):
         return pl.ds(pl.multiple_of(base + part * 1024 + color * 256, 256), 256)
@@ -157,9 +181,9 @@
     zz = [(ring(1), whole), (ring(-1), whole)]
     routes = (
         xs + [(side, whole)],
+        zz + [(right, upper), (left, lower)],
+        zz + [(right, upper), (left, lower)],
         zz + [(side, whole)],
-        xs + [(ring(1), upper), (ring(-1), lower)],
-        zz + [(right, upper), (left, lower)],
     )
     relays = []
     for f in range(4):
@@ -186,40 +210,61 @@
         b = jnp.broadcast_to(ref[d, row + 1 : row + 2, :], (64, 128))
         return jnp.concatenate([a, b], axis=0).astype(BF)
 
-    def pass_on(*which):
-        for d in which:
-            gk[d].wait_recv()
-            gkv[d].start()
-
-    pass_on(1, 7)
+    def pass_on(d, to):
+        gmk[d].wait_recv()
+        gk[d].wait_recv()
+        if to is not None:
+            gmk[to].start()
+            gk[to].start()
+        elif d == 3:
+            gmk[4].start()
+            gk[4].start()
+        else:
+            gk[0].start()
+        gkv[d].start()
+
+    pass_on(1, 2)
+    pass_on(7, 6)
+    gmq[1].wait_recv()
+    gmq[2].start()
     gq[1][0].wait_recv()
     gq[2][0].start()
+    gmq[3].wait_recv()
     gq[3][1].wait_recv()
     gq[2][1].start()
+    gmq[4].wait_recv()
+    gmq[5].start()
+    gmq[7].start()
     gq[4][0].wait_recv()
     gq[5][0].start()
     gq[7][0].start()
-    pass_on(2, 6)
+    pass_on(2, 3)
+    pass_on(6, 5)
     gq[4][1].wait_recv()
     gq[5][1].start()
     gq[7][1].start()
     gq[1][1].wait_recv()
     gq[3][0].wait_recv()
-    pass_on(3, 5)
+    pass_on(3, None)
+    pass_on(5, None)
+    gmq[2].wait_recv()
+    gmq[6].start()
     for i in range(2):
         gq[2][i].wait_recv()
         gq[6][i].start()
-    pass_on(4)
+    gmk[4].wait_recv()
+    gk[4].wait_recv()
+    gk[0].wait_recv()
+    gkv[4].start()
     for cp in own[:4]:
         cp.wait()
     for d in (0,) + ORDER:
         if d:
-            gmk[d].wait_recv()
             gkv[d].wait_recv()
         at = pl.ds(d * 128, 128)
         OH[at, :] = runs(MK, d, 2)
         KT[:, d * 128 : (d + 1) * 128] = KV[0, d].astype(F32).T.astype(BF)
-    for d in ORDER:
+    for d in (5, 6, 7):
         gmq[d].wait_recv()
 
     def rows_of(i, n):
@@ -349,6 +394,7 @@
         rc(dqf, dqx.at[i], x_s.at[i], x_r.at[i], dev)
         for i, dev in enumerate((mate, far, far_mate))
     ]
+    relays[0][2].wait_recv()
     for cp in (gx[2], gx[1], gx[0]):
         cp.start()
 
@@ -364,9 +410,8 @@
         cp.wait_recv()
     for cp in own[4:]:
         cp.wait()
-    for group in relays:
-        for cp in group:
-            cp.wait_recv()
+    for cp in relays[0][:2] + relays[1] + relays[2] + relays[3]:
+        cp.wait_recv()
     for cp in gx:
         cp.wait_recv()
     all_dq = jnp.concatenate([dqf[...], dqx[0], dqx[1], dqx[2]], axis=1)
@@ -410,7 +455,7 @@
         for cp in gq[d]:
             cp.wait_send()
         rc(dqs.at[d], dqr.at[d], dq_s.at[d], dq_r.at[d], owner_of(d)).wait_send()
-    for cp in wpush + gx + gh + [pair]:
+    for cp in wpush + gx + gh + [pair, gk[0]]:
         cp.wait_send()
     for f in range(4):
         for cp in relays[f] + list(over[f]):

time: 63.4 us -> 64.1 us (1.011)
  no operation moved by 1% of the time
where the time goes in v4:
time: 64.1 us; the launch traced here: 63.1 us
  Pallas kernels  62.1 us (97%)
  local copies, waits for them, and re-layouts  0.97 us (2%)
    pallas_call x1, Pallas kernels, on_device(): pl.pallas_call(kernel, out_shape=pltpu.VMEM((128, 4096), BF), in_specs=[s...  62.1 us

profile of v4, /device:TPU:1, one launch (start us, length us, event | category | flops | bytes accessed | tf_op | source)
XLA Modules:
  0.0 63.1 jit_solution(12675470050511558189)
XLA Ops:
  0.0 62.1 %shard_map.82 = bf16[128,4096]{1,0:T(8,128)(2,1)S(1)} custom-call(s32[128]{0:T(128)} %pos.1, s32[128]{0:T(128)} %doc.1, bf16[128,256]{1,0:T(8,128)(2,1)} %q.1, bf16[128,256]{1,0:T(8,128)(2,1)} %do.1, bf16[128,128]{1,0:T(8,128)(2,1)} %k.1, bf16[128,128]{1,0:T(8,128)(2,1)} %v.1, bf16[256,16384]{1,0:T(8,128)(2,1)} %wq.1, bf16[256,4096]{1,0:T(8,128)(2,1)} %wkv.1), custom_call_target="tpu_custom_call" | custom-call | tf_op jit(solution)/shard_map/pallas_call | solution.py:483
  62.1 1.0 %copy.10 = bf16[128,4096]{1,0:T(8,128)(2,1)} copy(bf16[128,4096]{1,0:T(8,128)(2,1)S(1)} %shard_map.82) | data formatting | bytes 2097152

commit v5 on v3

--- a/solution.py
+++ b/solution.py
@@ -99,6 +99,9 @@
     ORDER = (1, 7, 2, 6, 3, 5, 4)
     gk = {d: rc(k, KV.at[c, d], k_s.at[d], k_r.at[d], ring(d)) for d in ORDER}
     gv = {d: rc(v, KV.at[c, d], k_s.at[d], k_r.at[d], ring(d)) for d in ORDER}
+    halves = (pl.ds(0, 64), pl.ds(64, 64))
+    gk[4] = rc(KV.at[c, 3, halves[0]], KV.at[c, 4, halves[0]], k_s.at[4], k_r.at[4], ring(1))
+    gk[0] = rc(KV.at[c, 5, halves[1]], KV.at[c, 4, halves[1]], k_s.at[0], k_r.at[0], ring(-1))
     gkv = {d: rc(KV.at[c, d], KV.at[c, d], v_s.at[d], v_r.at[d], mate) for d in ORDER}
     gmk = {d: rc(meta, MK.at[d], mk_s.at[d], mk_r.at[d], ring(d)) for d in ORDER}
     gmq = {d: rc(meta, MQ.at[d], mq_s.at[d], mq_r.at[d], plane(d)) for d in ORDER}
@@ -119,12 +122,12 @@
 
     @pl.when(c == 0)
     def _():
-        for d in ORDER:
+        for d in ORDER[:6]:
             gk[d].start()
 
     @pl.when(c == 1)
     def _():
-        for d in ORDER:
+        for d in ORDER[:6]:
             gv[d].start()
 
     for d, i in ((1, 0), (3, 1), (4, 0), (1, 1), (3, 0), (4, 1)):
@@ -133,47 +136,54 @@
         gmk[d].start()
         gmq[d].start()
 
-    def colors(yy):
-        return ((x + 2 * yy) % 4, (z + 2 * yy) % 4, (x + 2 * z) % 4, (z + 2 * x) % 4)
-
-    def sub(part, color, base=0):
-        return pl.ds(pl.multiple_of(base + part * 1024 + color * 256, 256), 256)
-
-    mine_c, theirs_c = colors(yl), colors(1 - yl)
+    color = (z + 2 * x + 4 * yl) % 8
+    up, down = ring(1), ring(-1)
+    whole, upper, lower = pl.ds(512, 512), pl.ds(512, 256), pl.ds(768, 256)
+
+    def sub(f, shift, base=0):
+        return pl.ds(pl.multiple_of(base + f * 2048 + ((color + shift) % 8) * 256, 256), 256)
+
     over = []
-    for f in range(4):
+    for f in range(2):
         at = [(2 * (1 - u) + cc) * 4096 for cc in (c, 1 - c)]
-        into = sub(f, theirs_c[f])
-        over.append((
-            rc(wq.at[:, sub(f, theirs_c[f], at[0])], W.at[pl.ds(512, 256), into], cs.at[f, 0], cr.at[f, 0], cross),
-            rc(wq.at[:, sub(f, theirs_c[f], at[1])], W.at[pl.ds(768, 256), into], cs.at[f, 1], cr.at[f, 1], cross_mate),
-        ))
-    for pair_of in over:
-        for cp in pair_of:
-            cp.start()
-
-    whole, upper, lower = pl.ds(512, 512), pl.ds(512, 256), pl.ds(768, 256)
-    xs = [(right, whole), (left, whole)]
-    zz = [(ring(1), whole), (ring(-1), whole)]
-    routes = (
-        xs + [(side, whole)],
-        zz + [(side, whole)],
-        xs + [(ring(1), upper), (ring(-1), lower)],
-        zz + [(right, upper), (left, lower)],
-    )
-    relays = []
-    for f in range(4):
-        at = sub(f, mine_c[f])
-        relays.append([
-            rc(W.at[part, at], W.at[part, at], fs.at[f, i], fr.at[f, i], dev)
-            for i, (dev, part) in enumerate(routes[f])
+        into = sub(f, 4)
+        over.append([
+            rc(wq.at[:, sub(f, 4, at[0])], W.at[upper, into], cs.at[f, 0], cr.at[f, 0], cross),
+            rc(wq.at[:, sub(f, 4, at[1])], W.at[lower, into], cs.at[f, 1], cr.at[f, 1], cross_mate),
         ])
-
-    def relay(f):
-        for cp in over[f]:
-            cp.wait_recv()
-        for cp in relays[f]:
-            cp.start()
+    for cp in over[0] + over[1]:
+        cp.start()
+
+    def spread(f, i, part, shift, dev):
+        at = sub(f, shift)
+        return rc(W.at[part, at], W.at[part, at], fs.at[f, i], fr.at[f, i], dev)
+
+    near = [
+        [spread(f, i, whole, 0, dev) for i, dev in enumerate((right, left, up, down, side))]
+        for f in range(2)
+    ]
+    next_near = [
+        [spread(0, 5, whole, 2, down), spread(0, 6, whole, 6, up)],
+        [
+            spread(1, 5, upper, 1, side),
+            spread(1, 6, upper, 7, side),
+            spread(1, 7, lower, 1, left),
+            spread(1, 8, lower, 7, right),
+        ],
+    ]
+
+    def relay(step):
+        f = step % 2
+        if step < 2:
+            for cp in over[f]:
+                cp.wait_recv()
+            for cp in near[f]:
+                cp.start()
+        else:
+            for i in ((0, 1), (2, 3))[f]:
+                near[f][i].wait_recv()
+            for cp in next_near[f]:
+                cp.start()
 
     wpush = [rc(wq.at[:, cols(u, 1 - c)], W.at[pl.ds(256, 256)], w_s, w_r, mate)]
     for cp in wpush:
@@ -205,10 +215,17 @@
     gq[7][1].start()
     gq[1][1].wait_recv()
     gq[3][0].wait_recv()
-    pass_on(3, 5)
+    gk[3].wait_recv()
+    gk[4].start()
+    gkv[3].start()
+    gk[5].wait_recv()
+    gk[0].start()
+    gkv[5].start()
     for i in range(2):
         gq[2][i].wait_recv()
         gq[6][i].start()
+    relay(0)
+    gk[0].wait_recv()
     pass_on(4)
     for cp in own[:4]:
         cp.wait()
@@ -278,12 +295,14 @@
         {d: rc(stat.at[g], stat_all.at[d, g], st_s.at[d, g], st_r.at[d, g], plane(d)) for d in ORDER}
         for g in range(2)
     ]
-    relay(0)
     for g in range(2):
-        lax.fori_loop(0, 4, functools.partial(first, g), 0)
+        lax.fori_loop(0, 2, functools.partial(first, g), 0)
+        if g == 0:
+            relay(1)
+        lax.fori_loop(2, 4, functools.partial(first, g), 0)
         for d in ORDER:
             gs[g][d].start()
-        relay(1 + g)
+    relay(2)
 
     def merge(g):
         parts = [stat[g]]
@@ -330,13 +349,20 @@
     for g in range(2):
         merge(g)
         lax.fori_loop(0, 4, functools.partial(second, g), 0)
-        if g == 0:
-            relay(3)
 
     first_core = c == 0
     pair_s[...] = jnp.where(first_core, dv[...], dk[...]).astype(BF)
     pair = rc(pair_s, pair_r, pr_s, pr_r, mate)
     pair.start()
+
+    pair.wait_recv()
+    for d in range(8):
+        at = pl.ds(d * 128, 128)
+        zs[d] = (jnp.where(first_core, dk[at, :], dv[at, :]) + pair_r[at, :].astype(F32)).astype(BF)
+    relay(3)
+    gz = {d: rc(zs.at[d], zr.at[d], z_s.at[d], z_r.at[d], ring(-d)) for d in ORDER}
+    for d in ORDER:
+        gz[d].start()
 
     dqsum = dqs[0].astype(F32)
     for d in range(1, 8):
@@ -352,32 +378,6 @@
     for cp in (gx[2], gx[1], gx[0]):
         cp.start()
 
-    pair.wait_recv()
-    for d in range(8):
-        at = pl.ds(d * 128, 128)
-        zs[d] = (jnp.where(first_core, dk[at, :], dv[at, :]) + pair_r[at, :].astype(F32)).astype(BF)
-    gz = {d: rc(zs.at[d], zr.at[d], z_s.at[d], z_r.at[d], ring(-d)) for d in ORDER}
-    for d in ORDER:
-        gz[d].start()
-
-    for cp in wpush:
-        cp.wait_recv()
-    for cp in own[4:]:
-        cp.wait()
-    for group in relays:
-        for cp in group:
-            cp.wait_recv()
-    for cp in gx:
-        cp.wait_recv()
-    all_dq = jnp.concatenate([dqf[...], dqx[0], dqx[1], dqx[2]], axis=1)
-
-    def query_part(n, carry):
-        col = pl.ds(pl.multiple_of(n * 512, 512), 512)
-        acc[:, col] = mm(all_dq, W[:, col])
-        return carry
-
-    lax.fori_loop(0, 8, query_part, 0)
-
     ksum = zs[0].astype(F32)
     for d in range(1, 8):
         gz[d].wait_recv()
@@ -389,6 +389,23 @@
     ]
     for cp in gh:
         cp.start()
+    for cp in wpush:
+        cp.wait_recv()
+    for cp in own[4:]:
+        cp.wait()
+    for cp in near[0][2:] + near[1][:2] + near[1][4:] + next_near[0] + next_near[1]:
+        cp.wait_recv()
+    for cp in gx:
+        cp.wait_recv()
+    all_dq = jnp.concatenate([dqf[...], dqx[0], dqx[1], dqx[2]], axis=1)
+
+    def query_part(n, carry):
+        col = pl.ds(pl.multiple_of(n * 512, 512), 512)
+        acc[:, col] = mm(all_dq, W[:, col])
+        return carry
+
+    lax.fori_loop(0, 8, query_part, 0)
+
     for cp in gh:
         cp.wait_recv()
     mine = hs[...].astype(F32) + hr[1].astype(F32)
@@ -410,11 +427,10 @@
         for cp in gq[d]:
             cp.wait_send()
         rc(dqs.at[d], dqr.at[d], dq_s.at[d], dq_r.at[d], owner_of(d)).wait_send()
-    for cp in wpush + gx + gh + [pair]:
+    for cp in wpush + gx + gh + [pair, gk[0]]:
         cp.wait_send()
-    for f in range(4):
-        for cp in relays[f] + list(over[f]):
-            cp.wait_send()
+    for cp in over[0] + over[1] + near[0] + near[1] + next_near[0] + next_near[1]:
+        cp.wait_send()
 
 
 def on_device(queries, keys, values, dout, positions, doc_ids, w_query, w_kv):
@@ -434,7 +450,7 @@
     ]
     scratch += [dma((8,))] * 12 + [dma((8, 2))] * 2 + [dma((8,))] * 4
     scratch += [dma, dma, dma((3,)), dma((3,)), dma((3,)), dma((3,)), dma, dma]
-    scratch += [dma((4, 2)), dma((4, 2)), dma((4, 4)), dma((4, 4)), dma((6,))]
+    scratch += [dma((2, 2)), dma((2, 2)), dma((2, 9)), dma((2, 9)), dma((6,))]
     return pl.pallas_call(
         kernel,
         out_shape=pltpu.VMEM((128, 4096), BF),

time: 63.4 us -> 60.9 us (0.961); the launches traced: 62.5 us -> 60.8 us
  Pallas kernels: 61.5 us -> 59.9 us
    pallas_call x1, Pallas kernels: 61.5 us -> 59.9 us  [on_device(): pl.pallas_call(kernel, out_shape=pltpu.VMEM((128, 4096), BF), in_specs=[s...]
where the time goes in v5:
time: 60.9 us; the launch traced here: 60.8 us
  Pallas kernels  59.9 us (98%)
  local copies, waits for them, and re-layouts  0.97 us (2%)
    pallas_call x1, Pallas kernels, on_device(): pl.pallas_call(kernel, out_shape=pltpu.VMEM((128, 4096), BF), in_specs=[s...  59.9 us

profile of v5, /device:TPU:1, one launch (start us, length us, event | category | flops | bytes accessed | tf_op | source)
XLA Modules:
  0.0 60.8 jit_solution(676620217417440128)
XLA Ops:
  0.0 59.9 %shard_map.82 = bf16[128,4096]{1,0:T(8,128)(2,1)S(1)} custom-call(s32[128]{0:T(128)} %pos.1, s32[128]{0:T(128)} %doc.1, bf16[128,256]{1,0:T(8,128)(2,1)} %q.1, bf16[128,256]{1,0:T(8,128)(2,1)} %do.1, bf16[128,128]{1,0:T(8,128)(2,1)} %k.1, bf16[128,128]{1,0:T(8,128)(2,1)} %v.1, bf16[256,16384]{1,0:T(8,128)(2,1)} %wq.1, bf16[256,4096]{1,0:T(8,128)(2,1)} %wkv.1), custom_call_target="tpu_custom_call" | custom-call | tf_op jit(solution)/shard_map/pallas_call | solution.py:454
  59.9 1.0 %copy.10 = bf16[128,4096]{1,0:T(8,128)(2,1)} copy(bf16[128,4096]{1,0:T(8,128)(2,1)S(1)} %shard_map.82) | data formatting | bytes 2097152

commit v6 on v5

--- a/solution.py
+++ b/solution.py
@@ -186,8 +186,6 @@
                 cp.start()
 
     wpush = [rc(wq.at[:, cols(u, 1 - c)], W.at[pl.ds(256, 256)], w_s, w_r, mate)]
-    for cp in wpush:
-        cp.start()
     for cp in own[4:]:
         cp.start()
 
@@ -227,6 +225,8 @@
     relay(0)
     gk[0].wait_recv()
     pass_on(4)
+    for cp in wpush:
+        cp.start()
     for cp in own[:4]:
         cp.wait()
     for d in (0,) + ORDER:
@@ -235,7 +235,6 @@
             gkv[d].wait_recv()
         at = pl.ds(d * 128, 128)
         OH[at, :] = runs(MK, d, 2)
-        KT[:, d * 128 : (d + 1) * 128] = KV[0, d].astype(F32).T.astype(BF)
     for d in ORDER:
         gmq[d].wait_recv()
 
@@ -321,6 +320,8 @@
         coef[g, 0:4, :] = jnp.exp(mloc[g] - (big + jnp.log(tot)))
         coef[g, 4:8, :] = mix / tot
 
+    for d in range(8):
+        KT[:, d * 128 : (d + 1) * 128] = KV[0, d].astype(F32).T.astype(BF)
     dk[...] = jnp.zeros_like(dk)
     dv[...] = jnp.zeros_like(dv)
 
@@ -393,18 +394,24 @@
         cp.wait_recv()
     for cp in own[4:]:
         cp.wait()
-    for cp in near[0][2:] + near[1][:2] + near[1][4:] + next_near[0] + next_near[1]:
-        cp.wait_recv()
     for cp in gx:
         cp.wait_recv()
     all_dq = jnp.concatenate([dqf[...], dqx[0], dqx[1], dqx[2]], axis=1)
 
-    def query_part(n, carry):
-        col = pl.ds(pl.multiple_of(n * 512, 512), 512)
-        acc[:, col] = mm(all_dq, W[:, col])
-        return carry
-
-    lax.fori_loop(0, 8, query_part, 0)
+    def query_part(f, shifts):
+        for shift in shifts:
+            acc[:, sub(f, shift)] = mm(all_dq, W[:, sub(f, shift)])
+
+    for cp in near[0][2:]:
+        cp.wait_recv()
+    query_part(0, (0, 1, 2, 4, 6, 7))
+    for cp in near[1][:2] + near[1][4:]:
+        cp.wait_recv()
+    query_part(1, (0, 1, 2, 4, 6, 7))
+    for f in range(2):
+        for cp in next_near[f]:
+            cp.wait_recv()
+        query_part(f, (3, 5))
 
     for cp in gh:
         cp.wait_recv()
@@ -419,7 +426,7 @@
         out[:, col] = (acc[:, col] + mm(kvg, WK[:, col])).astype(BF)
         return carry
 
-    lax.fori_loop(0, 8, finish, 0)
+    lax.fori_loop(0, 8, finish, 0, unroll=2)
 
     for d in ORDER:
         for g in (gk, gkv, gmk, gmq, gs[0], gs[1], gz):

time: 60.9 us -> 59.6 us (0.979)
  Pallas kernels: 59.9 us -> 58.5 us
    pallas_call x1, Pallas kernels: 59.9 us -> 58.5 us  [on_device(): pl.pallas_call(kernel, out_shape=pltpu.VMEM((128, 4096), BF), in_specs=[s...]
where the time goes in v6:
time: 59.6 us; the launch traced here: 59.5 us
  Pallas kernels  58.5 us (98%)
  local copies, waits for them, and re-layouts  0.97 us (2%)
    pallas_call x1, Pallas kernels, on_device(): pl.pallas_call(kernel, out_shape=pltpu.VMEM((128, 4096), BF), in_specs=[s...  58.5 us

profile of v6, /device:TPU:1, one launch (start us, length us, event | category | flops | bytes accessed | tf_op | source)
XLA Modules:
  0.0 59.5 jit_solution(4658940233934410760)
XLA Ops:
  0.0 58.5 %shard_map.82 = bf16[128,4096]{1,0:T(8,128)(2,1)S(1)} custom-call(s32[128]{0:T(128)} %pos.1, s32[128]{0:T(128)} %doc.1, bf16[128,256]{1,0:T(8,128)(2,1)} %q.1, bf16[128,256]{1,0:T(8,128)(2,1)} %do.1, bf16[128,128]{1,0:T(8,128)(2,1)} %k.1, bf16[128,128]{1,0:T(8,128)(2,1)} %v.1, bf16[256,16384]{1,0:T(8,128)(2,1)} %wq.1, bf16[256,4096]{1,0:T(8,128)(2,1)} %wkv.1), custom_call_target="tpu_custom_call" | custom-call | tf_op jit(solution)/shard_map/pallas_call | solution.py:461
  58.5 1.0 %copy.10 = bf16[128,4096]{1,0:T(8,128)(2,1)} copy(bf16[128,4096]{1,0:T(8,128)(2,1)S(1)} %shard_map.82) | data formatting | bytes 2097152

commit v7 on v6

--- a/solution.py
+++ b/solution.py
@@ -165,10 +165,8 @@
     next_near = [
         [spread(0, 5, whole, 2, down), spread(0, 6, whole, 6, up)],
         [
-            spread(1, 5, upper, 1, side),
-            spread(1, 6, upper, 7, side),
-            spread(1, 7, lower, 1, left),
-            spread(1, 8, lower, 7, right),
+            spread(1, 5, whole, 1, left),
+            spread(1, 6, whole, 7, right),
         ],
     ]
 
@@ -295,13 +293,11 @@
         for g in range(2)
     ]
     for g in range(2):
-        lax.fori_loop(0, 2, functools.partial(first, g), 0)
-        if g == 0:
-            relay(1)
-        lax.fori_loop(2, 4, functools.partial(first, g), 0)
+        lax.fori_loop(0, 1, functools.partial(first, g), 0)
+        relay(1 + g)
+        lax.fori_loop(1, 4, functools.partial(first, g), 0)
         for d in ORDER:
             gs[g][d].start()
-    relay(2)
 
     def merge(g):
         parts = [stat[g]]

time: 59.6 us -> 56.8 us (0.953)
  Pallas kernels: 58.5 us -> 55.7 us
    pallas_call x1, Pallas kernels: 58.5 us -> 55.7 us  [on_device(): pl.pallas_call(kernel, out_shape=pltpu.VMEM((128, 4096), BF), in_specs=[s...]
where the time goes in v7:
time: 56.8 us; the launch traced here: 56.7 us
  Pallas kernels  55.7 us (98%)
  local copies, waits for them, and re-layouts  0.97 us (2%)
    pallas_call x1, Pallas kernels, on_device(): pl.pallas_call(kernel, out_shape=pltpu.VMEM((128, 4096), BF), in_specs=[s...  55.7 us

profile of v7, /device:TPU:1, one launch (start us, length us, event | category | flops | bytes accessed | tf_op | source)
XLA Modules:
  0.0 56.7 jit_solution(15273931424099507461)
XLA Ops:
  0.0 55.7 %shard_map.82 = bf16[128,4096]{1,0:T(8,128)(2,1)S(1)} custom-call(s32[128]{0:T(128)} %pos.1, s32[128]{0:T(128)} %doc.1, bf16[128,256]{1,0:T(8,128)(2,1)} %q.1, bf16[128,256]{1,0:T(8,128)(2,1)} %do.1, bf16[128,128]{1,0:T(8,128)(2,1)} %k.1, bf16[128,128]{1,0:T(8,128)(2,1)} %v.1, bf16[256,16384]{1,0:T(8,128)(2,1)} %wq.1, bf16[256,4096]{1,0:T(8,128)(2,1)} %wkv.1), custom_call_target="tpu_custom_call" | custom-call | tf_op jit(solution)/shard_map/pallas_call | solution.py:457
  55.7 1.0 %copy.10 = bf16[128,4096]{1,0:T(8,128)(2,1)} copy(bf16[128,4096]{1,0:T(8,128)(2,1)S(1)} %shard_map.82) | data formatting | bytes 2097152
